TPU v7x, 32 devices: a whole 2x2x4 slice. The times are simulated.
32 devices in a mesh: expert: 8 (over z, x), hidden: 4 (over y, core).
Axes of the slice: x: 2, y: 2, z: 4, core: 2. Of those that a mesh axis runs over, the one named last changes fastest.
Arguments:
- tokens: bfloat16 [16384, 768], P(('expert', 'hidden')), may hold values from -6 to 6
- doc_lengths: int32 [8, 3], P('expert'), may hold values from 1 to 1024, 2048 in all within a row
- expert_ids: int32 [16384, 2], P(('expert', 'hidden')), may hold values from 0 to 7, all different within a row; in each aligned block of 512 rows (0 to 511, 512 to 1023, ...) at most 160 rows name the same one
- gain_one: float32 [768], replicated, may hold values from 0.5 to 1.5
- shift_one: float32 [768], replicated, may hold values from -1.25 to 1.25
- w_query: bfloat16 [768, 768], replicated, may hold values from -0.21875 to 0.21875
- w_key: bfloat16 [768, 768], replicated, may hold values from -0.21875 to 0.21875
- w_value: bfloat16 [768, 768], replicated, may hold values from -0.21875 to 0.21875
- w_out: bfloat16 [768, 768], replicated, may hold values from -3.5 to 3.5
- gain_two: float32 [768], replicated, may hold values from 0.5 to 1.5
- shift_two: float32 [768], replicated, may hold values from -1.25 to 1.25
- w_router: bfloat16 [768, 8], replicated, may hold values from -0.21875 to 0.21875
- w_up: bfloat16 [8, 768, 3072], P('expert', None, 'hidden'), may hold values from -0.21875 to 0.21875
- w_down: bfloat16 [8, 3072, 768], P('expert', 'hidden'), may hold values from -0.109375 to 0.109375
- out_grad: bfloat16 [16384, 768], P(('expert', 'hidden')), may hold values from -6 to 6
Outputs:
- output: bfloat16 [16384, 768], P(('expert', 'hidden'))
- input_grad: bfloat16 [16384, 768], P(('expert', 'hidden'))
- gain_one_grad: float32 [768], replicated
- shift_one_grad: float32 [768], replicated
- w_query_grad: float32 [768, 768], replicated
- w_key_grad: float32 [768, 768], replicated
- w_value_grad: float32 [768, 768], replicated
- w_out_grad: float32 [768, 768], replicated
- gain_two_grad: float32 [768], replicated
- shift_two_grad: float32 [768], replicated
- w_router_grad: float32 [768, 8], replicated
- w_up_grad: float32 [8, 768, 3072], P('expert', None, 'hidden')
- w_down_grad: float32 [8, 3072, 768], P('expert', 'hidden')
- load: float32 [8], replicated
Inputs may be any that keep to these rules, and one draw needn't show every extreme that they name: `doc_lengths`: the lengths of a group's documents, in order; they sum to 2048 and the longest in every group is 1024. `expert_ids`: each token names 2 different experts; among the 512 tokens of one device no expert is named more than 160 times, and in every draw some expert is named exactly 160 times by one device.
All inputs are finite; a program needn't handle non-finite values.
Results may differ from a plain program's by a relative error of at most 0.019.
Values may be sent and summed in bfloat16 or wider, within the bound.
A program may use at most 192 MiB of HBM per device.

v0:
```python
from functools import partial

import jax
import jax.numpy as jnp
from jax import lax
from jax.experimental import pallas as pl
from jax.experimental.pallas import tpu as pltpu
from jax.sharding import PartitionSpec as P

HEAD_DIM = 64
HEADS = 12
EPSILON = 1e-05
SCALE = 0.125
MASKED = -1e30
BLOCK = 256
LONGEST = 1024
REACH = LONGEST // BLOCK + 1
LANES = 128
BF = jnp.bfloat16
F32 = jnp.float32
I32 = jnp.int32
MESH = pl.DeviceIdType.MESH
ANY = pl.BlockSpec(memory_space=pl.ANY)
SMEM = pl.BlockSpec(memory_space=pltpu.SMEM)
VMEM = pl.BlockSpec(memory_space=pltpu.VMEM)
DMA = pltpu.SemaphoreType.DMA
GELU_A = 0.7978845608028654
GELU_B = 0.044715


def mm(left, right):
    return jnp.dot(left, right, preferred_element_type=F32)


def mm_nt(left, right):
    return lax.dot_general(left, right, (((1,), (1,)), ((), ())), preferred_element_type=F32)


def mm_tn(left, right):
    return lax.dot_general(left, right, (((0,), (0,)), ((), ())), preferred_element_type=F32)


def iota(shape, axis):
    return lax.broadcasted_iota(I32, shape, axis)


def norm_parts(values):
    centred = values - jnp.mean(values, axis=-1, keepdims=True)
    inverse = lax.rsqrt(jnp.mean(centred * centred, axis=-1, keepdims=True) + EPSILON)
    return centred * inverse, inverse


def norm_back(grad_out, normed, inverse, gain):
    grad_normed = grad_out * gain
    first = jnp.mean(grad_normed, axis=-1, keepdims=True)
    second = jnp.mean(grad_normed * normed, axis=-1, keepdims=True)
    return inverse * (grad_normed - first - normed * second)


def split_two(value):
    high = value.astype(BF)
    return high, (value - high.astype(F32)).astype(BF)


def shape_of(shape, dtype):
    return jax.ShapeDtypeStruct(shape, dtype)


def greet(peers):
    barrier = pltpu.get_barrier_semaphore()
    for peer in peers:
        pl.semaphore_signal(barrier, inc=1, device_id=peer, device_id_type=MESH)
    pl.semaphore_wait(barrier, len(peers))


def remote(src, dst, send, recv, peer):
    return pltpu.make_async_remote_copy(
        src_ref=src, dst_ref=dst, send_sem=send, recv_sem=recv, device_id=peer, device_id_type=MESH
    )


def doc_bounds(docs):
    ends, at = [], 0
    for n in range(docs.shape[1] - 1):
        at = at + docs[0, n]
        ends.append(at)
    return ends


def start_of(place, ends):
    begin = jnp.zeros_like(place)
    for end in ends:
        begin = jnp.where(place >= end, end, begin)
    return begin


def lying(ref):
    return ref[...].reshape(1, ref.shape[0])


def aligned(at, size):
    return pl.ds(pl.multiple_of(at, size), size)


def find_slots(experts, capacity, ids, ids_t, pos, slot, count):
    rows = ids_t.shape[1]
    row = [ids_t[j : j + 1, :] for j in range(2)]
    tall = jnp.concatenate([r.astype(F32) for r in row] + [jnp.zeros((6, rows), F32)], axis=0)
    ids[...] = tall.T[:, 0:2].astype(I32)
    col = [ids[:, j : j + 1] for j in range(2)]
    lane = iota((rows, LANES), 1)
    hot = [(lane == c).astype(BF) for c in col]
    either = hot[0] + hot[1]
    below = (iota((rows, rows), 0) > iota((rows, rows), 1)).astype(BF)
    before = mm(below, either)
    wide = max(experts, 16)
    deep = iota((wide, rows), 0)
    hot_t = [(deep == r).astype(BF) for r in row]
    above = (iota((rows, rows), 0) < iota((rows, rows), 1)).astype(BF)
    before_t = mm(hot_t[0] + hot_t[1], above)
    count[...] = jnp.sum(either.astype(F32), axis=0, keepdims=True)
    flat_t = []
    for j in range(2):
        at = jnp.sum(hot[j].astype(F32) * before, axis=1, keepdims=True).astype(I32)
        pos[:, j : j + 1] = col[j] * capacity + at
        slot[:, j : j + 1] = at
        at_t = jnp.sum(hot_t[j].astype(F32) * before_t, axis=0, keepdims=True).astype(I32)
        flat_t.append(row[j] * capacity + at_t)
    return flat_t


def fill_slots(flat_t, source, out):
    total, rows = out.shape[0], source.shape[0]
    half = total // 2
    for n in range(2):
        place = iota((half, rows), 0) + n * half
        pick = ((place == flat_t[0]) | (place == flat_t[1])).astype(BF)
        out[pl.ds(n * half, half), :] = mm(pick, source).astype(BF)


def attend_block(heads, ends, i, span, first, qkv, keys, scores, kept, inverse):
    width = heads * HEAD_DIM
    base = i * BLOCK
    rows = aligned(base, BLOCK)
    q_pos = base + iota((1, BLOCK), 1)
    begin = start_of(q_pos, ends)
    queries = [
        qkv[n * HEAD_DIM : (n + 1) * HEAD_DIM, rows] * jnp.asarray(SCALE, BF) for n in range(heads)
    ]
    tops = [jnp.full((1, BLOCK), MASKED, F32)] * heads
    for k in range(span):
        part = aligned((first + k) * BLOCK, BLOCK)
        k_pos = (first + k) * BLOCK + iota((BLOCK, BLOCK), 0)
        allowed = (k_pos <= q_pos) & (k_pos >= begin)
        for n in range(heads):
            score = jnp.where(allowed, mm(keys[n, part, :], queries[n]), MASKED)
            scores[n, k] = score
            tops[n] = jnp.maximum(tops[n], jnp.max(score, axis=0, keepdims=True))
    result = []
    for n in range(heads):
        total = jnp.zeros((1, BLOCK), F32)
        acc = jnp.zeros((HEAD_DIM, BLOCK), F32)
        lo = 2 * width + n * HEAD_DIM
        for k in range(span):
            weight = jnp.exp(scores[n, k] - tops[n])
            total = total + jnp.sum(weight, axis=0, keepdims=True)
            value = qkv[lo : lo + HEAD_DIM, aligned((first + k) * BLOCK, BLOCK)]
            low = weight.astype(BF)
            kept[n, k] = low
            acc = acc + mm(value, low)
        whole = 1.0 / total
        inverse[n : n + 1, rows] = whole
        result.append((acc * whole).astype(BF))
    return result


def spans(i, body):
    @pl.when(i < 2)
    def _short():
        body(2, 0)

    @pl.when(i >= 2)
    def _long():
        body(REACH, (i - (REACH - 1)) * (i // (REACH - 1)))


def front_body(
    n_e,
    n_h,
    experts,
    capacity,
    padded,
    heads,
    chunks,
    docs,
    ids_t,
    g1,
    s1,
    g2,
    s2,
    w_router,
    tokens,
    out_grad,
    w_query,
    w_key,
    w_value,
    w_out,
    w_up,
    all_tokens,
    qkv_out,
    att_out,
    att_t_out,
    w_t_out,
    g_in,
    x_slots,
    ups,
    weights,
    ids,
    pos,
    slot,
    count,
    inverse,
    residual,
    gates,
    gate_rows,
    tv,
    gv,
    wv,
    wo,
    w_t,
    qkv,
    keys,
    scores,
    kept,
    att_v,
    att_in,
    g_slots,
    xs_v,
    own_sem,
    w_sem,
    save_sem,
    kept_sem,
    ty_s,
    ty_r,
    tc_s,
    tc_r,
    tf_s,
    tf_r,
    gs_s,
    gs_r,
    at_s,
    at_r,
    wy_s,
    wy_r,
    wc_s,
    wc_r,
    wf_s,
    wf_r,
):
    e, h = lax.axis_index("expert"), lax.axis_index("hidden")
    far = n_h // 2
    pair, core = h // 2, lax.rem(h, 2)
    mate = pair * 2 + 1 - core
    rows, model = tokens.shape
    width = heads * HEAD_DIM
    per_device = rows // BLOCK
    ends = doc_bounds(docs)

    def across(t):
        return lax.rem(pair + t, far) * 2 + core

    def origin(t):
        return lax.rem(pair + far - t, far) * 2 + core

    own_tokens = pltpu.make_async_copy(tokens, tv.at[h], own_sem.at[0])
    own_grad = pltpu.make_async_copy(out_grad, gv, own_sem.at[1])
    own_grad.start()
    own_tokens.start()
    w_loads = [
        pltpu.make_async_copy(w, wv.at[n], w_sem.at[n])
        for n, w in enumerate((w_query, w_key, w_value))
    ]
    w_loads.append(pltpu.make_async_copy(w_out, wo, w_sem.at[3]))
    for load in w_loads:
        load.start()
    greet(
        [{"hidden": lax.rem(h + step, n_h)} for step in range(1, n_h)]
        + [{"expert": lax.rem(e + step, n_e)} for step in range(1, n_e)]
    )

    piece = rows // chunks
    sends = []
    for k in range(chunks):
        part = pl.ds(k * piece, piece)
        for t in range(1, far):
            copy = remote(
                tokens.at[part],
                tv.at[h, part],
                ty_s.at[t, k],
                ty_r.at[t, k],
                {"hidden": across(t)},
            )
            copy.start()
            sends.append(copy)
    beside = remote(tokens, tv.at[h], tc_s, tc_r, {"hidden": mate})
    beside.start()
    sends.append(beside)

    flat_t = find_slots(experts, capacity, ids, ids_t, pos, slot, count)
    own_grad.wait()
    fill_slots(flat_t, gv[...], g_slots)
    for step in range(1, n_e):
        peer = lax.rem(e + step, n_e)
        copy = remote(
            g_slots.at[aligned(peer * capacity, capacity)],
            g_in.at[e],
            gs_s.at[step],
            gs_r.at[step],
            {"expert": peer},
        )
        copy.start()
        sends.append(copy)
    own_slots = pltpu.make_async_copy(
        g_slots.at[aligned(e * capacity, capacity)], g_in.at[e], own_sem.at[1]
    )
    own_slots.start()

    def pass_on(t, k):
        part = pl.ds(k * piece, piece)
        place = tv.at[origin(t), part]
        remote(place, place, ty_s.at[t, k], ty_r.at[t, k], {"hidden": across(t)}).wait_recv()
        copy = remote(place, place, tf_s.at[t, k], tf_r.at[t, k], {"hidden": mate})
        copy.start()
        sends.append(copy)

    todo = [(t, k) for k in range(chunks) for t in range(1, far)]
    third = -(-len(todo) // 4)

    def pass_some():
        for _ in range(min(third, len(todo))):
            pass_on(*todo.pop(0))

    pick = (iota((width, model), 1) == iota((width, model), 0) + h * width).astype(BF)
    for n in range(3):
        w_loads[n].wait()
        w_t[n * width : (n + 1) * width, :] = mm_nt(pick, wv[n]).astype(BF)
        if n == 1:
            pass_some()
    save_w = pltpu.make_async_copy(w_t, w_t_out, save_sem.at[0])
    save_w.start()

    def project(source):
        def one(b, _):
            normed, _unused = norm_parts(tv[source, aligned(b * BLOCK, BLOCK), :].astype(F32))
            hidden = (normed * lying(g1) + lying(s1)).astype(BF)
            block = mm_nt(w_t[...], hidden)
            cols = aligned(source * rows + b * BLOCK, BLOCK)
            qkv[:, cols] = block.astype(BF)
            for n in range(heads):
                lo = width + n * HEAD_DIM
                keys[n, cols, :] = block[lo : lo + HEAD_DIM].T.astype(BF)
            return 0

        lax.fori_loop(0, per_device, one, 0)

    pass_some()
    own_tokens.wait()
    project(h)
    pass_some()
    remote(tokens, tv.at[mate], tc_s, tc_r, {"hidden": mate}).wait_recv()
    project(mate)
    while todo:
        pass_some()

    deep = w_up.shape[1] // 2

    def up_part(k):
        return pl.ds(k * deep, deep)

    def up_across(k):
        for t in range(1, far):
            copy = remote(
                w_up.at[0, up_part(k)],
                ups.at[h, up_part(k)],
                wy_s.at[t, k],
                wy_r.at[t, k],
                {"hidden": across(t)},
            )
            copy.start()
            sends.append(copy)

    def up_onward(k):
        for t in range(1, far):
            place = ups.at[origin(t), up_part(k)]
            remote(place, place, wy_s.at[t, k], wy_r.at[t, k], {"hidden": mate}).wait_recv()
            copy = remote(place, place, wf_s.at[t, k], wf_r.at[t, k], {"hidden": mate})
            copy.start()
            sends.append(copy)

    own_up = pltpu.make_async_copy(w_up.at[0], ups.at[h], own_sem.at[2])
    own_up.start()
    up_beside = remote(w_up.at[0], ups.at[h], wc_s, wc_r, {"hidden": mate})
    up_beside.start()
    sends.append(up_beside)
    up_across(0)
    for t in range(1, far):
        project(origin(t))
    for t in range(1, far):
        there = lax.rem(pair + far - t, far) * 2 + 1 - core
        for k in range(chunks):
            place = tv.at[there, pl.ds(k * piece, piece)]
            remote(place, place, tf_s.at[t, k], tf_r.at[t, k], {"hidden": mate}).wait_recv()
        project(there)
    save_tokens = pltpu.make_async_copy(tv, all_tokens, save_sem.at[1])
    save_qkv = pltpu.make_async_copy(qkv, qkv_out, save_sem.at[2])
    save_tokens.start()
    save_qkv.start()

    inverse[...] = jnp.zeros_like(inverse)

    def device_at(n, sign):
        t, other = n // 2, lax.rem(n, 2)
        return lax.rem(pair + far + sign * t, far) * 2 + lax.rem(core + other, 2)

    def give_att(n):
        owner = device_at(n, 1)
        return remote(
            att_v.at[owner], att_in.at[h], at_s.at[n], at_r.at[n], {"hidden": owner}
        )

    def save_kept(i, turn):
        return pltpu.make_async_copy(kept.at[turn], weights.at[i], kept_sem.at[turn])

    def attend(at, _):
        n = n_h - 1 - at // per_device
        b = lax.rem(at, per_device)
        owner = device_at(n, 1)
        i = owner * per_device + b
        turn = lax.rem(at, 2)

        @pl.when(at >= 2)
        def _free():
            save_kept(i, turn).wait()

        def block(span, first):
            done = attend_block(
                heads, ends, i, span, first, qkv, keys, scores, kept.at[turn], inverse
            )
            for m in range(heads):
                lo = m * HEAD_DIM
                att_v[owner, lo : lo + HEAD_DIM, aligned(b * BLOCK, BLOCK)] = done[m]

        spans(i, block)
        save_kept(i, turn).start()

        @pl.when((b == per_device - 1) & (n > 0))
        def _give():
            give_att(n).start()

        return 0

    lax.fori_loop(0, n_h * per_device, attend, 0)
    up_onward(0)
    att_in[h] = att_v[h]
    save_att = pltpu.make_async_copy(att_v, att_out, save_sem.at[3])
    save_att.start()
    for n in range(n_h - 1, 0, -1):
        give_att(n).wait_recv()
    save_att_t = pltpu.make_async_copy(att_in, att_t_out, save_sem.at[4])
    save_att_t.start()

    up_across(1)

    w_loads[3].wait()
    res = tv[h].astype(F32) + mm_tn(att_in[...].reshape(model, rows), wo[...])
    residual[...] = res
    normed, _unused = norm_parts(res)
    hidden = (normed * lying(g2) + lying(s2)).astype(BF)
    fill_slots(flat_t, hidden, xs_v)
    save_x = [
        pltpu.make_async_copy(
            xs_v.at[pl.ds(n * capacity, capacity)], x_slots.at[n], save_sem.at[5 + n]
        )
        for n in range(experts)
    ]
    for save in save_x:
        save.start()
    logits = mm_nt(hidden, w_router[...])
    lane = iota((rows, experts), 1)
    chosen = [
        jnp.sum(jnp.where(lane == ids[:, j : j + 1], logits, 0.0), axis=1, keepdims=True)
        for j in range(2)
    ]
    top = jnp.maximum(chosen[0], chosen[1])
    raised = [jnp.exp(c - top) for c in chosen]
    both = raised[0] + raised[1]
    gate = [r / both for r in raised]
    for j in range(2):
        gates[:, j : j + 1] = gate[j]
    column = iota((rows, padded), 1)
    for n in range(experts):
        mix = jnp.zeros((rows, padded), F32)
        for j in range(2):
            here = jnp.where(ids[:, j : j + 1] == n, slot[:, j : j + 1], -1) == column
            mix = jnp.where(here, gate[j], mix)
        line = jnp.sum(mix, axis=0, keepdims=True)
        gate_rows[n] = jnp.broadcast_to(line, (8, padded))

    up_onward(1)
    place = ups.at[mate]
    remote(place, place, wc_s, wc_r, {"hidden": mate}).wait_recv()
    for k in range(2):
        for t in range(1, far):
            there = lax.rem(pair + far - t, far) * 2 + 1 - core
            place = ups.at[there, up_part(k)]
            remote(place, place, wf_s.at[t, k], wf_r.at[t, k], {"hidden": mate}).wait_recv()
    own_up.wait()
    for step in range(1, n_e):
        source = lax.rem(e + n_e - step, n_e)
        place = g_in.at[source]
        remote(place, place, gs_s.at[step], gs_r.at[step], {"expert": e}).wait_recv()
    own_slots.wait()
    for n in range(1, n_h):
        give_att(n).wait_send()
    for turn in range(2):
        save_kept(0, turn).wait()
    for copy in sends:
        copy.wait_send()
    for save in [save_w, save_tokens, save_qkv, save_att, save_att_t, *save_x]:
        save.wait()


def run_front(
    docs, ids_t, g1, s1, g2, s2, w_router, tokens, out_grad, ws, w_up, capacity, heads, cid
):
    n_e, n_h = lax.axis_size("expert"), lax.axis_size("hidden")
    experts = n_e * w_up.shape[0]
    rows, model = tokens.shape
    padded = -(-capacity // LANES) * LANES
    width, group, total = heads * HEAD_DIM, rows * n_h, experts * capacity
    far, chunks = n_h // 2, 8

    def pairs(*shape):
        return [DMA(shape), DMA(shape)]

    return pl.pallas_call(
        partial(front_body, n_e, n_h, experts, capacity, padded, heads, chunks),
        name="front",
        out_shape=[
            shape_of((n_h, rows, model), BF),
            shape_of((3 * width, group), BF),
            shape_of((n_h, width, rows), BF),
            shape_of((n_h, width, rows), BF),
            shape_of((3 * width, model), BF),
            shape_of((experts, capacity, model), BF),
            shape_of((experts, capacity, model), BF),
            shape_of((n_h, *w_up.shape[1:]), BF),
            shape_of((group // BLOCK, heads, REACH, BLOCK, BLOCK), BF),
            shape_of((rows, 2), I32),
            shape_of((rows, 2), I32),
            shape_of((rows, 2), I32),
            shape_of((1, LANES), F32),
            shape_of((8, group), F32),
            shape_of((rows, model), F32),
            shape_of((rows, 2), F32),
            shape_of((experts, 8, padded), F32),
        ],
        in_specs=[SMEM] + [VMEM] * 6 + [ANY] * 7,
        out_specs=[ANY] * 9 + [VMEM] * 8,
        scratch_shapes=[
            pltpu.VMEM((n_h, rows, model), BF),
            pltpu.VMEM((rows, model), BF),
            pltpu.VMEM((3, model, model), BF),
            pltpu.VMEM((model, model), BF),
            pltpu.VMEM((3 * width, model), BF),
            pltpu.VMEM((3 * width, group), BF),
            pltpu.VMEM((heads, group, HEAD_DIM), BF),
            pltpu.VMEM((heads, REACH, BLOCK, BLOCK), F32),
            pltpu.VMEM((2, heads, REACH, BLOCK, BLOCK), BF),
            pltpu.VMEM((n_h, width, rows), BF),
            pltpu.VMEM((n_h, width, rows), BF),
            pltpu.VMEM((total, model), BF),
            pltpu.VMEM((total, model), BF),
            DMA((4,)),
            DMA((4,)),
            DMA((5 + experts,)),
            DMA((2,)),
            *pairs(far, chunks),
            DMA,
            DMA,
            *pairs(far, chunks),
            *pairs(n_e),
            *pairs(n_h),
            *pairs(far, 2),
            DMA,
            DMA,
            *pairs(far, 2),
        ],
        compiler_params=pltpu.CompilerParams(
            collective_id=cid, has_side_effects=True, vmem_limit_bytes=58 << 20
        ),
    )(docs, ids_t, g1, s1, g2, s2, w_router, tokens, out_grad, *ws, w_up)


def moe_body(
    size,
    capacity,
    padded,
    per,
    x_slots,
    gate_rows,
    g_in,
    ups,
    w_down,
    dx_back,
    dg_back,
    y_out,
    dw_sum,
    dw_far,
    xv,
    gv,
    gates_v,
    up_v,
    down_v,
    act,
    dz,
    xg,
    dy,
    xg_t,
    dy_t,
    dxv,
    yv,
    dgv,
    y_acc,
    dx_acc,
    dw_box,
    load_sem,
    save_sem,
    wy_s,
    wy_r,
    wc_s,
    wc_r,
    wf_s,
    wf_r,
    dc_s,
    dc_r,
    df_s,
    df_r,
    g_sem,
    own_sem,
    xs_sem,
    xr_sem,
    gs_sem,
    gr_sem,
    ds_sem,
    dr_sem,
    ts_sem,
    tr_sem,
    out_sem,
):
    me, h = lax.axis_index("expert"), lax.axis_index("hidden")
    shards_n = ups.shape[0]
    far = shards_n // 2
    pair, core = h // 2, lax.rem(h, 2)
    mate = pair * 2 + 1 - core
    deep = w_down.shape[1] // 2
    tall = per * capacity
    steps = size // per

    def to_peer(p):
        return lax.rem(me + 3 * p, size)

    def from_peer(p):
        return lax.rem(me + 3 * (size - p), size)

    def rows_of(p):
        return pl.ds(pl.multiple_of(p * capacity, capacity), capacity)

    def send_x(p):
        peer = to_peer(p)
        return remote(
            x_slots.at[peer], xv.at[rows_of(p)], xs_sem.at[p], xr_sem.at[p], {"expert": peer}
        )

    def send_gate(p):
        peer = to_peer(p)
        return remote(
            gate_rows.at[peer], gates_v.at[p], gs_sem.at[p], gr_sem.at[p], {"expert": peer}
        )

    def send_dx(p):
        peer = from_peer(p)
        return remote(
            dxv.at[rows_of(p)], dx_back.at[me], ds_sem.at[p], dr_sem.at[p], {"expert": peer}
        )

    def send_dg(p):
        peer = from_peer(p)
        return remote(dgv.at[p], dg_back.at[me], ts_sem.at[p], tr_sem.at[p], {"expert": peer})

    def load_g(p):
        return pltpu.make_async_copy(g_in.at[from_peer(p)], gv.at[rows_of(p)], g_sem.at[p])

    def save_y(p):
        return pltpu.make_async_copy(yv.at[rows_of(p)], y_out.at[from_peer(p)], out_sem.at[p])

    own_x = pltpu.make_async_copy(x_slots.at[me], xv.at[rows_of(0)], own_sem.at[0])
    own_gate = pltpu.make_async_copy(gate_rows.at[me], gates_v.at[0], own_sem.at[1])
    own_dx = pltpu.make_async_copy(dxv.at[rows_of(0)], dx_back.at[me], own_sem.at[2])
    own_dg = pltpu.make_async_copy(dgv.at[0], dg_back.at[me], own_sem.at[3])
    load_up = pltpu.make_async_copy(ups, up_v, load_sem.at[0])
    load_down = pltpu.make_async_copy(w_down.at[0], down_v.at[h], load_sem.at[1])

    def half(k):
        return aligned(k * deep, deep)

    def down_across(t, k):
        there = {"hidden": lax.rem(pair + t, far) * 2 + core}
        return remote(
            w_down.at[0, half(k)], down_v.at[h, half(k)], wy_s.at[t, k], wy_r.at[t, k], there
        )

    def down_onward(t, k):
        place = down_v.at[lax.rem(pair + far - t, far) * 2 + core, half(k)]
        return remote(place, place, wf_s.at[t, k], wf_r.at[t, k], {"hidden": mate})

    down_beside = remote(w_down.at[0], down_v.at[h], wc_s, wc_r, {"hidden": mate})
    own_x.start()
    own_gate.start()
    for p in range(size):
        load_g(p).start()
    load_up.start()
    load_down.start()
    greet(
        [{"expert": lax.rem(me + step, size)} for step in range(1, size)]
        + [{"hidden": lax.rem(h + step, shards_n)} for step in range(1, shards_n)]
    )
    for p in range(1, size):
        send_x(p).start()
        send_gate(p).start()
    for k in range(2):
        for t in range(1, far):
            down_across(t, k).start()
    down_beside.start()
    own_x.wait()
    own_gate.wait()
    load_up.wait()
    load_down.wait()

    def step_body(step, _):
        base = step * per
        for s in range(per):

            @pl.when(base + s > 0)
            def _arrive(s=s):
                send_x(base + s).wait_recv()
                send_gate(base + s).wait_recv()

            load_g(base + s).wait()
        rows = pl.ds(pl.multiple_of(step * tall, tall), tall)
        x, g = xv[rows, :], gv[rows, :]
        y_acc[...] = jnp.zeros_like(y_acc)
        dx_acc[...] = jnp.zeros_like(dx_acc)

        def shard_body(n, _):
            t = n // 2
            beside = lax.rem(n, 2)
            c = lax.rem(pair + far - t, far) * 2 + lax.rem(core + beside, 2)

            @pl.when((step == 0) & (n == 1))
            def _beside():
                down_beside.wait_recv()

            @pl.when((step == 0) & (n >= 2) & (beside == 0))
            def _across():
                for k in range(2):
                    down_across(t, k).wait_recv()
                    down_onward(t, k).start()

            @pl.when((step == 0) & (n >= 2) & (beside == 1))
            def _onward():
                for k in range(2):
                    down_onward(t, k).wait_recv()

            z = mm(x, up_v[c])
            du = mm_nt(g, down_v[c])
            square = z * z
            curve = jnp.tanh(z * (GELU_A + GELU_A * GELU_B * square))
            plus = 0.5 + 0.5 * curve
            hidden = (z * plus).astype(BF)
            rise = GELU_A + 3.0 * GELU_A * GELU_B * square
            slope = plus + 0.5 * z * (1.0 - curve * curve) * rise
            back = (slope * du).astype(BF)
            act[c, rows, :] = hidden
            dz[c, rows, :] = back
            y_acc[...] += mm(hidden, down_v[c])
            dx_acc[...] += mm_nt(back, up_v[c])
            return 0

        lax.fori_loop(0, shards_n, shard_body, 0)
        dxv[rows, :] = dx_acc[...].astype(BF)
        y_low = y_acc[...].astype(BF)
        yv[rows, :] = y_low
        dots = jnp.sum(y_low.astype(F32) * g.astype(F32), axis=1, keepdims=True)
        for s in range(per):
            p = base + s
            part = slice(s * capacity, (s + 1) * capacity)
            tall_dots = jnp.broadcast_to(dots[part], (capacity, LANES))
            if padded > capacity:
                blank = jnp.zeros((padded - capacity, LANES), F32)
                tall_dots = jnp.concatenate([tall_dots, blank], axis=0)
            dgv[p] = tall_dots.T[0:8]

            @pl.when(p > 0)
            def _give(p=p):
                send_dx(p).start()
                send_dg(p).start()

            @pl.when(p == 0)
            def _keep():
                own_dx.start()
                own_dg.start()

            save_y(p).start()
        for s in range(per):
            p = base + s
            part = slice(s * capacity, (s + 1) * capacity)
            gate = gates_v[p].T[0:capacity, 0:1]
            xg[rows_of(p), :] = (x[part].astype(F32) * gate).astype(BF)
            dy[rows_of(p), :] = (g[part].astype(F32) * gate).astype(BF)
        return 0

    lax.fori_loop(0, steps, step_body, 0)

    total = size * capacity
    turn = 256
    for k in range(total // turn):
        rows = slice(k * turn, (k + 1) * turn)
        xg_t[:, rows] = xg[rows, :].astype(F32).T.astype(BF)
        dy_t[:, rows] = dy[rows, :].astype(F32).T.astype(BF)
    model = xg_t.shape[0]
    bands = model // turn

    for t in range(1, far):
        for k in range(2):
            down_across(t, k).wait_send()
            down_onward(t, k).wait_send()
    down_beside.wait_send()

    def give(which, step):
        source = (up_v, down_v)[which].at[lax.rem(pair + step, far) * 2 + 1 - core]
        return remote(
            source,
            dw_box.at[which, step],
            dc_s.at[which, step],
            dc_r.at[which, step],
            {"hidden": mate},
        )

    def keep(which, step):
        source = (up_v, down_v)[which].at[lax.rem(pair + step, far) * 2 + core]
        return pltpu.make_async_copy(source, dw_sum.at[which, step], save_sem.at[which, step])

    def cross(step):
        source = up_v.at[lax.rem(pair + step, far) * 2 + core, half(0)]
        there = {"hidden": lax.rem(pair + step, far) * 2 + core}
        return remote(source, dw_far.at[step - 1], df_s.at[step], df_r.at[step], there)

    def other_body(n, _):
        band, step = lax.rem(n, bands), lax.rem(n // bands + 1, far)
        c = lax.rem(pair + step, far) * 2 + 1 - core
        lines = aligned(band * turn, turn)
        up_v[c, lines, :] = mm(xg_t[lines, :], dz[c]).astype(BF)
        down_v[c, lines, :] = mm(dy_t[lines, :], act[c]).astype(BF)

        @pl.when(band == bands - 1)
        def _give():
            for which in range(2):
                give(which, step).start()

        return 0

    lax.fori_loop(0, far * bands, other_body, 0)

    def own_body(n, _):
        band, step = lax.rem(n, bands), lax.rem(n // bands + 1, far)
        c = lax.rem(pair + step, far) * 2 + core

        @pl.when(band == 0)
        def _take():
            for which in range(2):
                give(which, step).wait_recv()

        lines = aligned(band * turn, turn)
        up = mm(xg_t[lines, :], dz[c]) + dw_box[0, step, lines, :].astype(F32)
        down = mm(dy_t[lines, :], act[c]) + dw_box[1, step, lines, :].astype(F32)
        up_v[c, lines, :] = up.astype(BF)
        down_v[c, lines, :] = down.astype(BF)

        @pl.when(band == bands - 1)
        def _keep():
            for which in range(2):
                keep(which, step).start()

        @pl.when((band == bands - 1) & (step > 0))
        def _cross():
            cross(step).start()

        return 0

    lax.fori_loop(0, far * bands, own_body, 0)
    for p in range(1, size):
        send_x(p).wait_send()
        send_gate(p).wait_send()
        send_dx(p).wait()
        send_dg(p).wait()
    for p in range(size):
        save_y(p).wait()
    own_dx.wait()
    own_dg.wait()
    for step in range(far):
        for which in range(2):
            give(which, step).wait_send()
            keep(which, step).wait()
    for step in range(1, far):
        cross(step).wait()


def run_experts(x_slots, gate_rows, g_in, ups, w_down, cid):
    size = lax.axis_size("expert")
    experts, capacity, model = x_slots.shape
    padded = gate_rows.shape[2]
    shards_n, _unused, width = ups.shape
    total = experts * capacity
    per = 1
    while per * 2 * capacity <= 320 and size % (per * 2) == 0:
        per *= 2
    tall = per * capacity
    rows2 = (total, model)
    return pl.pallas_call(
        partial(moe_body, size, capacity, padded, per),
        name="experts",
        out_shape=[
            shape_of(x_slots.shape, BF),
            shape_of(gate_rows.shape, F32),
            shape_of(x_slots.shape, BF),
            shape_of((2, shards_n // 2, model, width), BF),
            shape_of((shards_n // 2 - 1, model // 2, width), BF),
        ],
        in_specs=[ANY] * 5,
        out_specs=[ANY] * 5,
        scratch_shapes=[
            pltpu.VMEM(rows2, BF),
            pltpu.VMEM(rows2, BF),
            pltpu.VMEM(gate_rows.shape, F32),
            pltpu.VMEM((shards_n, model, width), BF),
            pltpu.VMEM((shards_n, width, model), BF),
            pltpu.VMEM((shards_n, total, width), BF),
            pltpu.VMEM((shards_n, total, width), BF),
            pltpu.VMEM(rows2, BF),
            pltpu.VMEM(rows2, BF),
            pltpu.VMEM((model, total), BF),
            pltpu.VMEM((model, total), BF),
            pltpu.VMEM(rows2, BF),
            pltpu.VMEM(rows2, BF),
            pltpu.VMEM(gate_rows.shape, F32),
            pltpu.VMEM((tall, model), F32),
            pltpu.VMEM((tall, model), F32),
            pltpu.VMEM((2, shards_n // 2, model, width), BF),
            DMA((2,)),
            DMA((2, shards_n // 2)),
            DMA((shards_n // 2, 2)),
            DMA((shards_n // 2, 2)),
            DMA,
            DMA,
            DMA((shards_n // 2, 2)),
            DMA((shards_n // 2, 2)),
            DMA((2, shards_n // 2)),
            DMA((2, shards_n // 2)),
            DMA((shards_n // 2,)),
            DMA((shards_n // 2,)),
            DMA((size,)),
            DMA((4,)),
        ]
        + [DMA((size,))] * 9,
        compiler_params=pltpu.CompilerParams(
            collective_id=cid, has_side_effects=True, vmem_limit_bytes=60 << 20
        ),
        cost_estimate=pl.CostEstimate(
            flops=12 * total * model * width * shards_n, bytes_accessed=40 << 20, transcendentals=0
        ),
    )(x_slots, gate_rows, g_in, ups, w_down)


def tail_body(
    n_e,
    n_h,
    chunks,
    dh,
    w_all,
    small,
    tokens,
    gain,
    d_res,
    residual,
    gates,
    pos,
    y_back,
    input_grad,
    output,
    full,
    total,
    mine,
    beside,
    across,
    passing,
    x_box,
    z_box,
    w_mid,
    piece,
    small_mid,
    small_h,
    small_e,
    mine_sem,
    cs_sem,
    cr_sem,
    as_sem,
    ar_sem,
    ws_sem,
    wr_sem,
    vs_sem,
    vr_sem,
    hs_sem,
    hr_sem,
    es_sem,
    er_sem,
    keep_sem,
    zs_sem,
    zr_sem,
    xs_sem,
    xr_sem,
    ys_sem,
    yr_sem,
    ms_sem,
    mr_sem,
):
    e, h = lax.axis_index("expert"), lax.axis_index("hidden")
    far, high = n_h // 2, n_e // 2
    pair, core = h // 2, lax.rem(h, 2)
    eh, el = e // 2, lax.rem(e, 2)
    mate = pair * 2 + 1 - core
    greet(
        [{"expert": lax.rem(e + step, n_e)} for step in range(1, n_e)]
        + [{"hidden": lax.rem(h + step, n_h)} for step in range(1, n_h)]
    )
    w_sends, w_order = [], list(range(1, high)) + [0]
    for step in w_order:
        there = lax.rem(eh + step, high)
        copy = remote(
            w_all.at[there * 2 + 1 - el],
            x_box.at[step],
            ws_sem.at[step],
            wr_sem.at[step],
            {"expert": eh * 2 + 1 - el},
        )
        copy.start()
        w_sends.append(copy)
    rows = dh.shape[1] // chunks
    core_sends = {}
    for step in list(range(1, far)) + [0]:
        there = lax.rem(pair + step, far)
        for k in range(chunks):
            part = pl.ds(k * rows, rows)
            copy = remote(
                dh.at[there * 2 + 1 - core, part],
                beside.at[step, part],
                cs_sem.at[step, k],
                cr_sem.at[step, k],
                {"hidden": mate},
            )
            copy.start()
            core_sends[step, k] = copy
    loads = []
    for step in range(far):
        there = lax.rem(pair + step, far)
        load = pltpu.make_async_copy(dh.at[there * 2 + core], mine.at[step], mine_sem.at[step])
        load.start()
        loads.append(load)
    small_sends = []
    for at in range(n_h - 1):
        peer = lax.rem(h + 1 + at, n_h)
        copy = remote(small, small_h.at[at], hs_sem.at[at], hr_sem.at[at], {"hidden": peer})
        copy.start()
        small_sends.append(copy)
    v_sends = []
    for at, step in enumerate(w_order[:-1]):
        there = lax.rem(eh + step, high) * 2 + el
        w_sends[at].wait_recv()
        w_mid[step - 1] = (w_all[there].astype(F32) + x_box[step].astype(F32)).astype(BF)
        copy = remote(
            w_mid.at[step - 1],
            z_box.at[step - 1],
            vs_sem.at[step],
            vr_sem.at[step],
            {"expert": there},
        )
        copy.start()
        v_sends.append(copy)
    for load in loads:
        load.wait()
    far_sends = []
    for step in range(1, far):
        there = lax.rem(pair + step, far)
        for k in range(chunks):
            part = pl.ds(k * rows, rows)
            core_sends[step, k].wait_recv()
            both = mine[step, part, :].astype(F32) + beside[step, part, :].astype(F32)
            passing[step - 1, part, :] = both.astype(BF)
            copy = remote(
                passing.at[step - 1, part],
                across.at[step - 1, part],
                as_sem.at[step - 1, k],
                ar_sem.at[step - 1, k],
                {"hidden": there * 2 + core},
            )
            copy.start()
            far_sends.append(copy)
    for copy in small_sends:
        copy.wait_recv()
    summed = small[...]
    for at in range(n_h - 1):
        summed = summed + small_h[at]
    small_mid[...] = summed
    small_out = []
    for at in range(n_e - 1):
        peer = lax.rem(e + 1 + at, n_e)
        copy = remote(small_mid, small_e.at[at], es_sem.at[at], er_sem.at[at], {"expert": peer})
        copy.start()
        small_out.append(copy)
    w_sends[-1].wait_recv()
    acc = w_all[e].astype(F32) + x_box[0].astype(F32)
    for at, copy in enumerate(v_sends):
        copy.wait_recv()
        acc = acc + z_box[at].astype(F32)
    piece[...] = acc.astype(BF)
    keep = pltpu.make_async_copy(piece, full.at[h, e], keep_sem)
    keep.start()
    started = []

    def slot(eh_of, el_of, pair_of, core_of):
        return full.at[pair_of * 2 + core_of, eh_of * 2 + el_of]

    def back(step, size, place):
        return lax.rem(place + size - step, size)

    def give_z(source):
        for s in range(1, high):
            there = lax.rem(eh + s, high) * 2 + el
            copy = remote(
                source, slot(eh, el, pair, core), zs_sem.at[s], zr_sem.at[s], {"expert": there}
            )
            copy.start()
            started.append(copy)

    def z_arrival(s):
        place = slot(back(s, high, eh), el, pair, core)
        return place, remote(place, place, zs_sem.at[s], zr_sem.at[s], {"expert": e})

    def give_x(source, s):
        target = slot(back(s, high, eh), el, pair, core)
        copy = remote(
            source, target, xs_sem.at[s], xr_sem.at[s], {"expert": eh * 2 + 1 - el}
        )
        copy.start()
        started.append(copy)

    def x_arrival(s):
        place = slot(back(s, high, eh), 1 - el, pair, core)
        return place, remote(place, place, xs_sem.at[s], xr_sem.at[s], {"expert": e})

    def give_y(source, s, flag):
        target = slot(back(s, high, eh), el if flag == 0 else 1 - el, pair, core)
        for t in range(1, far):
            there = lax.rem(pair + t, far) * 2 + core
            at = 2 * s + flag
            copy = remote(
                source, target, ys_sem.at[t, at], yr_sem.at[t, at], {"hidden": there}
            )
            copy.start()
            started.append(copy)

    def y_arrival(t, s, flag):
        other = el if flag == 0 else 1 - el
        place = slot(back(s, high, eh), other, back(t, far, pair), core)
        at = 2 * s + flag
        return place, remote(place, place, ys_sem.at[t, at], yr_sem.at[t, at], {"hidden": h})

    def give_mate(source, t, s, flag):
        other = el if flag == 0 else 1 - el
        target = slot(back(s, high, eh), other, back(t, far, pair), core)
        at = 2 * s + flag
        copy = remote(source, target, ms_sem.at[t, at], mr_sem.at[t, at], {"hidden": mate})
        copy.start()
        started.append(copy)

    def mate_arrival(t, s, flag):
        other = el if flag == 0 else 1 - el
        place = slot(back(s, high, eh), other, back(t, far, pair), 1 - core)
        at = 2 * s + flag
        return place, remote(place, place, ms_sem.at[t, at], mr_sem.at[t, at], {"hidden": h})

    give_z(piece)
    give_x(piece, 0)
    give_y(piece, 0, 0)
    give_mate(piece, 0, 0, 0)
    for s in range(1, high):
        place, arrival = z_arrival(s)
        arrival.wait_recv()
        give_x(place, s)
        give_y(place, s, 0)
        give_mate(place, 0, s, 0)
    for s in range(high):
        place, arrival = x_arrival(s)
        arrival.wait_recv()
        give_y(place, s, 1)
        give_mate(place, 0, s, 1)
    place_of = iota((residual.shape[0], y_back.shape[0]), 1)
    result = residual[...]
    for j in range(2):
        pick = (place_of == pos[:, j : j + 1]).astype(BF)
        result = result + gates[:, j : j + 1] * mm(pick, y_back[...])
    output[...] = result.astype(BF)
    for copy in small_out:
        copy.wait_recv()
    summed = small_mid[...]
    for at in range(n_e - 1):
        summed = summed + small_e[at]
    total[...] = summed
    for k in range(chunks):
        part = pl.ds(k * rows, rows)
        core_sends[0, k].wait_recv()
    for copy in far_sends:
        copy.wait_recv()
    grad = mine[0].astype(F32) + beside[0].astype(F32)
    for step in range(far - 1):
        grad = grad + across[step].astype(F32)
    normed, inverse = norm_parts(tokens[...].astype(F32))
    input_grad[...] = (d_res[...] + norm_back(grad, normed, inverse, lying(gain))).astype(BF)
    for t in range(1, far):
        for s in range(high):
            for flag in range(2):
                place, arrival = y_arrival(t, s, flag)
                arrival.wait_recv()
                give_mate(place, t, s, flag)
    for t in range(far):
        for s in range(high):
            for flag in range(2):
                _place, arrival = mate_arrival(t, s, flag)
                arrival.wait_recv()
    keep.wait()
    for copy in started + w_sends + v_sends + small_sends + small_out + far_sends:
        copy.wait_send()
    for copy in core_sends.values():
        copy.wait_send()


def run_tail(dh, w_all, small, tokens, gain, d_res, residual, gates, pos, y_back, cid):
    n_e, n_h = lax.axis_size("expert"), lax.axis_size("hidden")
    far, high = n_h // 2, n_e // 2
    chunks = 4
    _unused, rows, model = dh.shape
    piece = w_all.shape[1:]
    return pl.pallas_call(
        partial(tail_body, n_e, n_h, chunks),
        name="tail",
        out_shape=[
            shape_of((rows, model), BF),
            shape_of((rows, model), BF),
            shape_of((n_h, n_e, *piece), BF),
            shape_of(small.shape, F32),
        ],
        in_specs=[ANY] + [VMEM] * 9,
        out_specs=[VMEM, VMEM, ANY, VMEM],
        scratch_shapes=[
            pltpu.VMEM((far, rows, model), BF),
            pltpu.VMEM((far, rows, model), BF),
            pltpu.VMEM((far - 1, rows, model), BF),
            pltpu.VMEM((far - 1, rows, model), BF),
            pltpu.VMEM((high, *piece), BF),
            pltpu.VMEM((high - 1, *piece), BF),
            pltpu.VMEM((high - 1, *piece), BF),
            pltpu.VMEM(piece, BF),
            pltpu.VMEM(small.shape, F32),
            pltpu.VMEM((n_h - 1, *small.shape), F32),
            pltpu.VMEM((n_e - 1, *small.shape), F32),
            DMA((far,)),
            DMA((far, chunks)),
            DMA((far, chunks)),
            DMA((far - 1, chunks)),
            DMA((far - 1, chunks)),
            DMA((high,)),
            DMA((high,)),
            DMA((high,)),
            DMA((high,)),
            DMA((n_h - 1,)),
            DMA((n_h - 1,)),
            DMA((n_e - 1,)),
            DMA((n_e - 1,)),
            DMA,
            DMA((high,)),
            DMA((high,)),
            DMA((high,)),
            DMA((high,)),
            DMA((far, n_e)),
            DMA((far, n_e)),
            DMA((far, n_e)),
            DMA((far, n_e)),
        ],
        compiler_params=pltpu.CompilerParams(
            collective_id=cid, has_side_effects=True, vmem_limit_bytes=56 << 20
        ),
    )(dh, w_all, small, tokens, gain, d_res, residual, gates, pos, y_back)


def turn_body(
    width,
    experts,
    full,
    dw,
    small,
    input_grad,
    output,
    q_out,
    k_out,
    v_out,
    o_out,
    up_out,
    down_out,
    g1_out,
    s1_out,
    g2_out,
    s2_out,
    router_out,
    input_out,
    output_out,
):
    @pl.when(pl.program_id(0) == 0)
    def _begin():
        input_out[...] = input_grad[...]
        output_out[...] = output[...]
        for n, out in enumerate((g1_out, s1_out, g2_out, s2_out)):
            out[...] = small[n : n + 1, :].reshape(out.shape)
        router_out[...] = small[8 : 8 + experts, :]

    for n, out in enumerate((q_out, k_out, v_out)):
        part = full[:, n * width : (n + 1) * width, :].astype(F32)
        out[...] = part.reshape(-1, part.shape[2]).T
    part = full[:, 3 * width :, :].astype(F32)
    o_out[...] = part.reshape(-1, part.shape[2])
    trained = jnp.where(lax.axis_index("expert") >= experts // 2, 1.0, 0.0)
    up_out[...] = dw[0] * trained
    down_out[...] = dw[1].T * trained


def turn_weights(full, dw, small, input_grad, output, width, experts):
    n_h, deep, model = full.shape
    cols = 256
    across = pl.BlockSpec((cols, model), lambda i: (i, 0))
    down = pl.BlockSpec((model, cols), lambda i: (0, i))
    flat = pl.BlockSpec((model,), lambda i: (0,))
    whole = pl.BlockSpec(output.shape, lambda i: (0, 0))
    square = shape_of((model, model), F32)
    return pl.pallas_call(
        partial(turn_body, width, experts),
        name="turn_weights",
        grid=(model // cols,),
        out_shape=[square] * 6
        + [shape_of((model,), F32)] * 4
        + [
            shape_of((experts, model), F32),
            shape_of(input_grad.shape, BF),
            shape_of(output.shape, BF),
        ],
        in_specs=[
            pl.BlockSpec((n_h, deep, cols), lambda i: (0, 0, i)),
            pl.BlockSpec((2, model, cols), lambda i: (0, 0, i)),
            pl.BlockSpec(small.shape, lambda i: (0, 0)),
            whole,
            whole,
        ],
        out_specs=[across, across, across, down, down, across]
        + [flat] * 4
        + [pl.BlockSpec((experts, model), lambda i: (0, 0)), whole, whole],
        compiler_params=pltpu.CompilerParams(
            dimension_semantics=("arbitrary",), vmem_limit_bytes=60 << 20
        ),
        cost_estimate=pl.CostEstimate(flops=0, bytes_accessed=24 << 20, transcendentals=0),
    )(full, dw, small, input_grad, output)


def attend_back(
    heads, i, span, first, qkv, given, centre, kept, values, dq_acc, dk_acc, dv_acc
):
    width = heads * HEAD_DIM
    rows = aligned(i * BLOCK, BLOCK)
    dq_acc[...] = jnp.zeros_like(dq_acc)
    queries = [
        qkv[n * HEAD_DIM : (n + 1) * HEAD_DIM, rows] * jnp.asarray(SCALE, BF) for n in range(heads)
    ]
    for k in range(span):
        part = aligned((first + k) * BLOCK, BLOCK)
        for n in range(heads):
            here = slice(n * HEAD_DIM, (n + 1) * HEAD_DIM)
            weight = kept[n, k]
            d_weight = mm(values[n, part, :], given[n])
            d_score = (weight.astype(F32) * (d_weight - centre[n])).astype(BF)
            dv_acc[here, part] += mm_nt(given[n], weight)
            dk_acc[here, part] += mm_nt(queries[n], d_score)
            lo = width + n * HEAD_DIM
            dq_acc[here, :] += mm(qkv[lo : lo + HEAD_DIM, part], d_score)


def back_body(
    n_e,
    n_h,
    experts,
    capacity,
    padded,
    heads,
    ids,
    slot,
    pos,
    gates,
    count,
    g1,
    s1,
    g2,
    s2,
    w_router,
    inverse,
    dg_rows,
    dx_back,
    y_out,
    dw_sum,
    dw_far,
    out_grad,
    residual,
    all_tokens,
    qkv_in,
    att_in,
    att_t_in,
    w_out,
    w_t_in,
    weights,
    y_back,
    d_hidden,
    d_res,
    w_all,
    small,
    dw_own,
    dxv,
    gv,
    res_v,
    tv,
    qkv,
    att_v,
    att_t,
    wo,
    w_t,
    d_att_v,
    d_att,
    wo_box,
    wo_far,
    kept,
    values,
    dq_acc,
    dk_acc,
    dv_acc,
    d_qkv,
    w_acc,
    dw_mine,
    dw_across,
    load_sem,
    save_sem,
    dw_sem,
    kept_sem,
    y_own,
    y_s,
    y_r,
    at_s,
    at_r,
    wo_s,
    wo_r,
    wf_s,
    wf_r,
    da_s,
    da_r,
):
    e, h = lax.axis_index("expert"), lax.axis_index("hidden")
    far = n_h // 2
    pair, core = h // 2, lax.rem(h, 2)
    mate = pair * 2 + 1 - core
    rows, model = out_grad.shape
    width = heads * HEAD_DIM
    group = rows * n_h
    per_device = rows // BLOCK
    blocks = group // BLOCK
    sends = []

    loads = [
        pltpu.make_async_copy(source, target, load_sem.at[n])
        for n, (source, target) in enumerate(
            (
                (residual, res_v),
                (dx_back, dxv),
                (out_grad, gv),
                (w_out, wo),
                (att_t_in, att_t),
                (qkv_in, qkv),
                (att_in, att_v),
                (all_tokens, tv),
                (w_t_in, w_t),
            )
        )
    ]
    for load in loads:
        load.start()
    greet(
        [{"hidden": lax.rem(h + step, n_h)} for step in range(1, n_h)]
        + [{"expert": lax.rem(e + step, n_e)} for step in range(1, n_e)]
    )
    load_dw = pltpu.make_async_copy(dw_sum.at[:, 0], dw_mine, dw_sem.at[0])
    load_dw.start()
    deep = dw_mine.shape[1] // 2
    load_far = pltpu.make_async_copy(
        dw_far, dw_across.at[0, :, pl.ds(0, deep)], dw_sem.at[1]
    )
    load_far.start()

    def dw_across_copy(which, step, k):
        part = pl.ds(k * deep, deep)
        return remote(
            dw_sum.at[which, step, part],
            dw_across.at[which, step - 1, part],
            da_s.at[which, step, k],
            da_r.at[which, step, k],
            {"hidden": lax.rem(pair + step, far) * 2 + core},
        )

    def dw_send(which, k):
        for step in range(1, far):
            dw_across_copy(which, step, k).start()

    for step in range(1, n_e):
        peer = lax.rem(e + step, n_e)
        copy = remote(y_out.at[peer], y_back.at[e], y_s.at[step], y_r.at[step], {"expert": peer})
        copy.start()
        sends.append(copy)
    own_y = pltpu.make_async_copy(y_out.at[e], y_back.at[e], y_own)
    own_y.start()

    for load in loads[:3]:
        load.wait()
    normed, spread = norm_parts(res_v[...])
    hidden = (normed * lying(g2) + lying(s2)).astype(BF)
    gate = [gates[:, j : j + 1] for j in range(2)]
    column = iota((rows, padded), 1)
    dot_of = []
    for j in range(2):
        mix = jnp.zeros((rows, padded), F32)
        for n in range(experts):
            here = jnp.where(ids[:, j : j + 1] == n, slot[:, j : j + 1], -1) == column
            mix = jnp.where(here, dg_rows[n, 0:1, :], mix)
        dot_of.append(jnp.sum(mix, axis=1, keepdims=True))
    mean = gate[0] * dot_of[0] + gate[1] * dot_of[1]
    lane = iota((rows, experts), 1)
    d_logits = jnp.zeros((rows, experts), F32)
    for j in range(2):
        d_logits = jnp.where(lane == ids[:, j : j + 1], gate[j] * (dot_of[j] - mean), d_logits)
    high, low = split_two(d_logits)
    grad = mm(high, w_router[...]) + mm(low, w_router[...])
    small[...] = jnp.zeros_like(small)
    small[8 : 8 + experts, :] = mm_tn(high, hidden) + mm_tn(low, hidden)
    small[4:5, 0:LANES] = count[...]
    place = iota((rows, experts * capacity), 1)
    for j in range(2):
        pick = (place == pos[:, j : j + 1]).astype(BF)
        grad = grad + gate[j] * mm(pick, dxv[...])
    small[2:3, :] = jnp.sum(grad * normed, axis=0, keepdims=True)
    small[3:4, :] = jnp.sum(grad, axis=0, keepdims=True)
    d_resid = gv[...].astype(F32) + norm_back(grad, normed, spread, lying(g2))
    d_res[...] = d_resid
    branch = d_resid.astype(BF)
    loads[3].wait()

    def device_at(n, sign):
        t, other = n // 2, lax.rem(n, 2)
        return lax.rem(pair + far + sign * t, far) * 2 + lax.rem(core + other, 2)

    def give_att(n):
        owner = device_at(n, 1)
        return remote(
            d_att_v.at[owner], d_att.at[h], at_s.at[n], at_r.at[n], {"hidden": owner}
        )

    for n in range(n_h - 1, -1, -1):
        owner = device_at(n, 1)
        block = mm_nt(wo[owner], branch).astype(BF)
        if n == 0:
            d_att[h] = block
        else:
            d_att_v[owner] = block
            give_att(n).start()
    loads[4].wait()
    for t in range(n_h):
        owner = lax.rem(h + t, n_h)
        wo[owner] = mm(att_t[owner], branch).astype(BF)
    for step in list(range(1, far)) + [0]:
        copy = remote(
            wo.at[lax.rem(pair + step, far) * 2 + 1 - core],
            wo_box.at[step],
            wo_s.at[step],
            wo_r.at[step],
            {"hidden": mate},
        )
        copy.start()
        sends.append(copy)
    def give_wo(step):
        target = lax.rem(pair + step, far) * 2 + core
        return remote(
            wo.at[target],
            wo_far.at[step - 1],
            wf_s.at[step],
            wf_r.at[step],
            {"hidden": target},
        )

    for load in loads[5:]:
        load.wait()

    def load_kept(i, turn):
        return pltpu.make_async_copy(weights.at[i], kept.at[turn], kept_sem.at[turn])

    def block_at(at):
        owner = device_at(at // per_device, 1)
        return owner, owner * per_device + lax.rem(at, per_device)

    load_kept(block_at(0)[1], 0).start()
    dk_acc[...] = jnp.zeros_like(dk_acc)
    dv_acc[...] = jnp.zeros_like(dv_acc)

    def turn_values(i, _):
        cols = aligned(i * BLOCK, BLOCK)
        for n in range(heads):
            lo = 2 * width + n * HEAD_DIM
            values[n, cols, :] = qkv[lo : lo + HEAD_DIM, cols].astype(F32).T.astype(BF)
        return 0

    lax.fori_loop(0, blocks, turn_values, 0)

    def over_queries(at, _):
        owner, i = block_at(at)
        turn = lax.rem(at, 2)

        @pl.when(at + 1 < blocks)
        def _next():
            load_kept(block_at(at + 1)[1], 1 - turn).start()

        @pl.when((at >= per_device) & (lax.rem(at, per_device) == 0))
        def _arrive():
            n = at // per_device
            source = lax.rem(far - n // 2, far) * 2 + lax.rem(n, 2)
            give_att(source).wait_recv()

        @pl.when(at == per_device)
        def _weights():
            for step in range(1, far):
                there = wo_box.at[step]
                target = lax.rem(pair + step, far) * 2 + core
                remote(there, there, wo_s.at[step], wo_r.at[step], {"hidden": mate}).wait_recv()
                both = wo[target].astype(F32) + wo_box[step].astype(F32)
                wo[target] = both.astype(BF)
                give_wo(step).start()
            dw_send(0, 1)
            dw_send(1, 0)
            dw_send(1, 1)

        load_kept(i, turn).wait()
        cols = aligned(lax.rem(at, per_device) * BLOCK, BLOCK)
        rows_i = aligned(i * BLOCK, BLOCK)
        given, centre = [], []
        for n in range(heads):
            here = slice(n * HEAD_DIM, (n + 1) * HEAD_DIM)
            scaled = d_att[owner, here, cols].astype(F32) * inverse[n : n + 1, rows_i]
            given.append(scaled.astype(BF))
            product = att_v[owner, here, cols].astype(F32) * scaled
            centre.append(jnp.sum(product, axis=0, keepdims=True))

        def block(span, first):
            attend_back(
                heads,
                i,
                span,
                first,
                qkv,
                given,
                centre,
                kept.at[turn],
                values,
                dq_acc,
                dk_acc,
                dv_acc,
            )

        spans(i, block)
        d_qkv[0:width, rows_i] = (dq_acc[...] * SCALE).astype(BF)
        return 0

    lax.fori_loop(0, blocks, over_queries, 0)
    w_acc[...] = jnp.zeros_like(w_acc)

    def finish(i, _):
        cols = aligned(i * BLOCK, BLOCK)
        d_qkv[width : 2 * width, cols] = dk_acc[:, cols].astype(BF)
        d_qkv[2 * width :, cols] = dv_acc[:, cols].astype(BF)
        block = d_qkv[:, cols]
        grad = mm_tn(block, w_t[...])
        inner = aligned(lax.rem(i, per_device) * BLOCK, BLOCK)
        normed, _unused = norm_parts(tv[i // per_device, inner, :].astype(F32))
        tv[i // per_device, inner, :] = grad.astype(BF)
        small[0:1, :] += jnp.sum(grad * normed, axis=0, keepdims=True)
        small[1:2, :] += jnp.sum(grad, axis=0, keepdims=True)
        hidden = (normed * lying(g1) + lying(s1)).astype(BF)
        w_acc[...] += mm(block, hidden)
        return 0

    lax.fori_loop(0, blocks, finish, 0)
    save_dh = pltpu.make_async_copy(tv, d_hidden, save_sem)
    save_dh.start()
    w_all[0 : 3 * width, :] = w_acc[...].astype(BF)
    there = wo_box.at[0]
    remote(there, there, wo_s.at[0], wo_r.at[0], {"hidden": mate}).wait_recv()
    total = wo[h].astype(F32) + wo_box[0].astype(F32)
    for step in range(1, far):
        give_wo(step).wait_recv()
        total = total + wo_far[step - 1].astype(F32)
    w_all[3 * width :, :] = total.astype(BF)
    load_dw.wait()
    load_far.wait()
    for which in range(2):
        for step in range(1, far):
            for k in range(1 - which, 2):
                dw_across_copy(which, step, k).wait()

        def add_all(n, _, which=which):
            band = aligned(n * 96, 96)
            both = dw_mine[which, band, :].astype(F32)
            for step in range(1, far):
                both = both + dw_across[which, step - 1, band, :].astype(F32)
            dw_own[which, band, :] = both
            return 0

        lax.fori_loop(0, dw_mine.shape[1] // 96, add_all, 0)
    for step in range(1, n_e):
        there = y_back.at[lax.rem(e + n_e - step, n_e)]
        remote(there, there, y_s.at[step], y_r.at[step], {"expert": e}).wait_recv()
    own_y.wait()
    save_dh.wait()
    for n in range(1, n_h):
        give_att(n).wait_send()
    for step in range(1, far):
        give_wo(step).wait_send()
    for copy in sends:
        copy.wait_send()


def run_back(
    ids,
    slot,
    pos,
    gates,
    count,
    g1,
    s1,
    g2,
    s2,
    w_router,
    inverse,
    dg_rows,
    dx_back,
    y_out,
    dw_sum,
    dw_far,
    out_grad,
    residual,
    all_tokens,
    qkv,
    att,
    att_t,
    w_out,
    w_t,
    weights,
    cid,
):
    n_e, n_h = lax.axis_size("expert"), lax.axis_size("hidden")
    experts, capacity, model = y_out.shape
    padded = dg_rows.shape[2]
    rows = out_grad.shape[0]
    width = w_t.shape[0] // 3
    heads = width // HEAD_DIM
    group, far = rows * n_h, n_h // 2
    shard = dw_sum.shape[2:]
    tall = 8 + experts

    def pairs(*shape):
        return [DMA(shape), DMA(shape)]

    return pl.pallas_call(
        partial(back_body, n_e, n_h, experts, capacity, padded, heads),
        name="back",
        out_shape=[
            shape_of(y_out.shape, BF),
            shape_of((n_h, rows, model), BF),
            shape_of((rows, model), F32),
            shape_of((4 * width, model), BF),
            shape_of((tall, model), F32),
            shape_of((2, *shard), F32),
        ],
        in_specs=[VMEM] * 12 + [ANY] * 13,
        out_specs=[ANY] * 2 + [VMEM] * 4,
        scratch_shapes=[
            pltpu.VMEM((experts * capacity, model), BF),
            pltpu.VMEM((rows, model), BF),
            pltpu.VMEM((rows, model), F32),
            pltpu.VMEM((n_h, rows, model), BF),
            pltpu.VMEM((3 * width, group), BF),
            pltpu.VMEM((n_h, width, rows), BF),
            pltpu.VMEM((n_h, width, rows), BF),
            pltpu.VMEM((n_h, width, model), BF),
            pltpu.VMEM((3 * width, model), BF),
            pltpu.VMEM((n_h, width, rows), BF),
            pltpu.VMEM((n_h, width, rows), BF),
            pltpu.VMEM((far, width, model), BF),
            pltpu.VMEM((far - 1, width, model), BF),
            pltpu.VMEM((2, heads, REACH, BLOCK, BLOCK), BF),
            pltpu.VMEM((heads, group, HEAD_DIM), BF),
            pltpu.VMEM((width, BLOCK), F32),
            pltpu.VMEM((width, group), F32),
            pltpu.VMEM((width, group), F32),
            pltpu.VMEM((3 * width, group), BF),
            pltpu.VMEM((3 * width, model), F32),
            pltpu.VMEM((2, *shard), BF),
            pltpu.VMEM((2, far - 1, *shard), BF),
            DMA((9,)),
            DMA,
            DMA((2,)),
            DMA((2,)),
            DMA,
            *pairs(n_e),
            *pairs(n_h),
            *pairs(far),
            *pairs(far),
            *pairs(2, far, 2),
        ],
        compiler_params=pltpu.CompilerParams(
            collective_id=cid, has_side_effects=True, vmem_limit_bytes=60 << 20
        ),
    )(
        ids,
        slot,
        pos,
        gates,
        count,
        g1,
        s1,
        g2,
        s2,
        w_router,
        inverse,
        dg_rows,
        dx_back.reshape(experts * capacity, model),
        y_out,
        dw_sum,
        dw_far,
        out_grad,
        residual,
        all_tokens,
        qkv,
        att,
        att_t,
        w_out.reshape(n_h, width, model),
        w_t,
        weights,
    )


def shards(
    tokens,
    doc_lengths,
    expert_ids,
    gain_one,
    shift_one,
    w_query,
    w_key,
    w_value,
    w_out,
    gain_two,
    shift_two,
    w_router,
    w_up,
    w_down,
    out_grad,
):
    rows, model = tokens.shape
    n_expert, n_hidden = lax.axis_size("expert"), lax.axis_size("hidden")
    experts = n_expert * w_up.shape[0]
    capacity = max(2, rows * 2 * 5 // (4 * experts))
    capacity = -(-capacity // 16) * 16
    total = experts * capacity
    heads = HEADS // n_hidden
    width = heads * HEAD_DIM
    g1, s1, g2, s2 = gain_one, shift_one, gain_two, shift_two
    router_t = w_router.T

    (
        all_tokens,
        qkv,
        att,
        att_t,
        w_t,
        g_in,
        x_slots,
        ups,
        weights,
        ids,
        pos,
        slot,
        count,
        inverse,
        residual,
        gates,
        gate_rows,
    ) = run_front(
        doc_lengths,
        expert_ids.T,
        g1,
        s1,
        g2,
        s2,
        router_t,
        tokens,
        out_grad,
        (w_query, w_key, w_value, w_out),
        w_up,
        capacity,
        heads,
        1,
    )
    dx_back, dg_back, y_out, dw_sum, dw_far = run_experts(
        x_slots, gate_rows, g_in, ups, w_down, 2
    )
    y_back, d_hidden, d_res, w_all, small, dw_own = run_back(
        ids,
        slot,
        pos,
        gates,
        count,
        g1,
        s1,
        g2,
        s2,
        router_t,
        inverse,
        dg_back,
        dx_back,
        y_out,
        dw_sum,
        dw_far,
        out_grad,
        residual,
        all_tokens,
        qkv,
        att,
        att_t,
        w_out,
        w_t,
        weights,
        3,
    )
    input_grad, output, full, small = run_tail(
        d_hidden,
        w_all.reshape(n_expert, 4 * width // n_expert, model),
        small,
        tokens,
        g1,
        d_res,
        residual,
        gates,
        pos,
        y_back.reshape(total, model),
        4,
    )
    scale = experts / (rows * n_expert * n_hidden * 2)
    turned = turn_weights(
        full.reshape(n_hidden, 4 * width, model),
        dw_own,
        small,
        input_grad,
        output,
        width,
        experts,
    )
    w_grads, (up_grad, down_grad) = turned[:4], turned[4:6]
    gain_one_grad, shift_one_grad, gain_two_grad, shift_two_grad = turned[6:10]
    router_grad, input_grad, output = turned[10:]
    return (
        output,
        input_grad,
        gain_one_grad,
        shift_one_grad,
        *w_grads,
        gain_two_grad,
        shift_two_grad,
        router_grad.T,
        up_grad[None],
        down_grad[None],
        small[4, :experts] * scale,
    )


def solution(mesh):
    in_specs = (
        P(("expert", "hidden"), None),
        P("expert", None),
        P(("expert", "hidden"), None),
        P(),
        P(),
        P(),
        P(),
        P(),
        P(),
        P(),
        P(),
        P(),
        P("expert", None, "hidden"),
        P("expert", "hidden", None),
        P(("expert", "hidden"), None),
    )
    out_specs = (
        P(("expert", "hidden"), None),
        P(("expert", "hidden"), None),
        P(),
        P(),
        P(),
        P(),
        P(),
        P(),
        P(),
        P(),
        P(),
        P("expert", None, "hidden"),
        P("expert", "hidden", None),
        P(),
    )
    return jax.shard_map(shards, mesh=mesh, in_specs=in_specs, out_specs=out_specs, check_vma=False)
```

profile of v0, /device:TPU:17, one launch (start us, length us, event | category | flops | bytes accessed | tf_op | source)
XLA Modules:
  0.0 323.9 jit_solution(6684103105239944818)
XLA Ops:
  0.6 63.2 %front.1 = (bf16[4,512,768]{2,1,0:T(8,128)(2,1)}, bf16[576,2048]{1,0:T(8,128)(2,1)}, bf16[4,192,512]{2,1,0:T(8,128)(2,1)}, bf16[4,192,512]{2,1,0:T(8,128)(2,1)},...) custom-call(s32[1,3]{1,0:T(1,128)} %docs.1, ...), custom_call_target="tpu_custom_call" | custom-call | tf_op jit(solution)/shard_map/front/pallas_call | solution.py:546
  63.9 90.7 %experts.1 = (bf16[8,160,768]{2,1,0:T(8,128)(2,1)}, f32[8,8,256]{2,1,0:T(8,128)}, bf16[8,160,768]{2,1,0:T(8,128)(2,1)}, bf16[2,2,768,768]{3,2,1,0:T(8,128)(2,1)}, bf16[1,384,768]{2,1,0:T(8,128)(2,1)}) custom-call(bf16[8,160,768]{2,1,0:T(8,128)(2,1)} %get-tuple-element.65.x_slots, f32[8,8,256]{2,1,0:T(8,128)} %get-tuple-element.66.gate_rows, ...), custom_call_target="tpu_custom_call" | custom-call | flops 36238786560 | bytes 41943040 | tf_op jit(solution)/shard_map/experts/pallas_call | solution.py:940
  154.6 86.4 %back.1 = (bf16[8,160,768]{2,1,0:T(8,128)(2,1)}, bf16[4,512,768]{2,1,0:T(8,128)(2,1)}, f32[512,768]{1,0:T(8,128)}, bf16[768,768]{1,0:T(8,128)(2,1)}, f32[16,768]{1,0:T(8,128)}, /*index=5*/f32[2,768,768]{2,1,0:T(8,128)}) custom-call(s32[512,2]{1,0:T(8,128)} %get-tuple-element.59.ids, s32[512,2]{1,0:T(8,128)} %get-tuple-element.60.slot, ...), custom_call_target="tpu_custom_call" | custom-call | tf_op jit(solution)/shard_map/back/pallas_call | solution.py:1818
  241.0 71.1 %tail.1 = (bf16[512,768]{1,0:T(8,128)(2,1)}, bf16[512,768]{1,0:T(8,128)(2,1)}, bf16[4,8,96,768]{3,2,1,0:T(8,128)(2,1)}, f32[16,768]{1,0:T(8,128)}) custom-call(bf16[4,512,768]{2,1,0:T(8,128)(2,1)} %get-tuple-element.81.dh, bf16[8,96,768]{2,1,0:T(8,128)(2,1)} %bitcast.16, f32[16,768]{1,0:T(8,128)} %get-tuple-element.83.small, bf16[512,768]{1,0:T(8,128)(2,1)} %tokens.3, ...), custom_call_target="tpu_custom_call" | custom-call | tf_op jit(solution)/shard_map/tail/pallas_call | solution.py:1273
  312.1 1.2 multiply_bitcast_fusion
  313.3 10.4 %turn_weights.1 = (f32[768,768]{1,0:T(8,128)}, f32[768,768]{1,0:T(8,128)}, f32[768,768]{1,0:T(8,128)}, f32[768,768]{1,0:T(8,128)}, f32[768,768]{1,0:T(8,128)}, /...) custom-call(bf16[4,768,768]{2,1,0:T(8,128)(2,1)} %bitcast.12, ...), custom_call_target="tpu_custom_call" | custom-call | bytes 25165824 | tf_op jit(solution)/shard_map/turn_weights/pallas_call | solution.py:1373
where the time goes:
time: 326 us; the launch traced here: 324 us
  Pallas kernels  322 us (99%)
    pallas_call x1, Pallas kernels, run_experts(): pl.pallas_call(partial(moe_body, size, capacity, padded, per), name='expe...  90.7 us
    pallas_call x1, Pallas kernels, run_back(): pl.pallas_call(partial(back_body, n_e, n_h, experts, capacity, padded, he...  86.4 us
    pallas_call x1, Pallas kernels, run_tail(): pl.pallas_call(partial(tail_body, n_e, n_h, chunks), name='tail', out_sha...  71.1 us
    pallas_call x1, Pallas kernels, run_front(): pl.pallas_call(partial(front_body, n_e, n_h, experts, capacity, padded, h...  63.2 us
    pallas_call x1, Pallas kernels, turn_weights(): pl.pallas_call(partial(turn_body, width, experts), name='turn_weights', g...  10.4 us

commit v1 on v0

--- a/solution.py
+++ b/solution.py
@@ -667,42 +667,46 @@
     tall = per * capacity
     steps = size // per
 
-    def to_peer(p):
-        return lax.rem(me + 3 * p, size)
-
-    def from_peer(p):
-        return lax.rem(me + 3 * (size - p), size)
+    middle = size // 2
+
+    def peer_at(p):
+        mask = jnp.where(p < 2, p, jnp.where(p < 2 + middle, p - 2 + middle, p - middle))
+        peer, bit = 0, 1
+        while bit < size:
+            peer = peer + lax.rem(me // bit + mask // bit, 2) * bit
+            bit *= 2
+        return peer
 
     def rows_of(p):
         return pl.ds(pl.multiple_of(p * capacity, capacity), capacity)
 
     def send_x(p):
-        peer = to_peer(p)
+        peer = peer_at(p)
         return remote(
             x_slots.at[peer], xv.at[rows_of(p)], xs_sem.at[p], xr_sem.at[p], {"expert": peer}
         )
 
     def send_gate(p):
-        peer = to_peer(p)
+        peer = peer_at(p)
         return remote(
             gate_rows.at[peer], gates_v.at[p], gs_sem.at[p], gr_sem.at[p], {"expert": peer}
         )
 
     def send_dx(p):
-        peer = from_peer(p)
+        peer = peer_at(p)
         return remote(
             dxv.at[rows_of(p)], dx_back.at[me], ds_sem.at[p], dr_sem.at[p], {"expert": peer}
         )
 
     def send_dg(p):
-        peer = from_peer(p)
+        peer = peer_at(p)
         return remote(dgv.at[p], dg_back.at[me], ts_sem.at[p], tr_sem.at[p], {"expert": peer})
 
     def load_g(p):
-        return pltpu.make_async_copy(g_in.at[from_peer(p)], gv.at[rows_of(p)], g_sem.at[p])
+        return pltpu.make_async_copy(g_in.at[peer_at(p)], gv.at[rows_of(p)], g_sem.at[p])
 
     def save_y(p):
-        return pltpu.make_async_copy(yv.at[rows_of(p)], y_out.at[from_peer(p)], out_sem.at[p])
+        return pltpu.make_async_copy(yv.at[rows_of(p)], y_out.at[peer_at(p)], out_sem.at[p])
 
     own_x = pltpu.make_async_copy(x_slots.at[me], xv.at[rows_of(0)], own_sem.at[0])
     own_gate = pltpu.make_async_copy(gate_rows.at[me], gates_v.at[0], own_sem.at[1])
@@ -735,7 +739,7 @@
         [{"expert": lax.rem(me + step, size)} for step in range(1, size)]
         + [{"hidden": lax.rem(h + step, shards_n)} for step in range(1, shards_n)]
     )
-    for p in range(1, size):
+    for p in range(1, middle):
         send_x(p).start()
         send_gate(p).start()
     for k in range(2):
@@ -770,6 +774,15 @@
             @pl.when((step == 0) & (n == 1))
             def _beside():
                 down_beside.wait_recv()
+
+            @pl.when((step == 0) & (n == 2))
+            def _second_half():
+                for p in range(1, middle):
+                    send_x(p).wait_send()
+                    send_gate(p).wait_send()
+                for p in range(middle, size):
+                    send_x(p).start()
+                    send_gate(p).start()
 
             @pl.when((step == 0) & (n >= 2) & (beside == 0))
             def _across():
@@ -909,9 +922,10 @@
         return 0
 
     lax.fori_loop(0, far * bands, own_body, 0)
-    for p in range(1, size):
+    for p in range(middle, size):
         send_x(p).wait_send()
         send_gate(p).wait_send()
+    for p in range(1, size):
         send_dx(p).wait()
         send_dg(p).wait()
     for p in range(size):
@@ -1325,6 +1339,7 @@
 def turn_body(
     width,
     experts,
+    scale,
     full,
     dw,
     small,
@@ -1343,6 +1358,7 @@
     router_out,
     input_out,
     output_out,
+    load_out,
 ):
     @pl.when(pl.program_id(0) == 0)
     def _begin():
@@ -1351,6 +1367,7 @@
         for n, out in enumerate((g1_out, s1_out, g2_out, s2_out)):
             out[...] = small[n : n + 1, :].reshape(out.shape)
         router_out[...] = small[8 : 8 + experts, :]
+        load_out[...] = small[4:5, 0:experts].reshape(experts) * scale
 
     for n, out in enumerate((q_out, k_out, v_out)):
         part = full[:, n * width : (n + 1) * width, :].astype(F32)
@@ -1358,20 +1375,20 @@
     part = full[:, 3 * width :, :].astype(F32)
     o_out[...] = part.reshape(-1, part.shape[2])
     trained = jnp.where(lax.axis_index("expert") >= experts // 2, 1.0, 0.0)
-    up_out[...] = dw[0] * trained
-    down_out[...] = dw[1].T * trained
-
-
-def turn_weights(full, dw, small, input_grad, output, width, experts):
+    up_out[...] = dw[0].astype(F32) * trained
+    down_out[...] = dw[1].astype(F32).T * trained
+
+
+def turn_weights(full, dw, small, input_grad, output, width, experts, scale):
     n_h, deep, model = full.shape
-    cols = 256
+    cols = 128
     across = pl.BlockSpec((cols, model), lambda i: (i, 0))
     down = pl.BlockSpec((model, cols), lambda i: (0, i))
     flat = pl.BlockSpec((model,), lambda i: (0,))
     whole = pl.BlockSpec(output.shape, lambda i: (0, 0))
     square = shape_of((model, model), F32)
     return pl.pallas_call(
-        partial(turn_body, width, experts),
+        partial(turn_body, width, experts, scale),
         name="turn_weights",
         grid=(model // cols,),
         out_shape=[square] * 6
@@ -1380,6 +1397,7 @@
             shape_of((experts, model), F32),
             shape_of(input_grad.shape, BF),
             shape_of(output.shape, BF),
+            shape_of((experts,), F32),
         ],
         in_specs=[
             pl.BlockSpec((n_h, deep, cols), lambda i: (0, 0, i)),
@@ -1390,7 +1408,8 @@
         ],
         out_specs=[across, across, across, down, down, across]
         + [flat] * 4
-        + [pl.BlockSpec((experts, model), lambda i: (0, 0)), whole, whole],
+        + [pl.BlockSpec((experts, model), lambda i: (0, 0)), whole, whole]
+        + [pl.BlockSpec((experts,), lambda i: (0,))],
         compiler_params=pltpu.CompilerParams(
             dimension_semantics=("arbitrary",), vmem_limit_bytes=60 << 20
         ),
@@ -1551,6 +1570,7 @@
         for step in range(1, far):
             dw_across_copy(which, step, k).start()
 
+    dw_send(0, 1)
     for step in range(1, n_e):
         peer = lax.rem(e + step, n_e)
         copy = remote(y_out.at[peer], y_back.at[e], y_s.at[step], y_r.at[step], {"expert": peer})
@@ -1681,7 +1701,6 @@
                 both = wo[target].astype(F32) + wo_box[step].astype(F32)
                 wo[target] = both.astype(BF)
                 give_wo(step).start()
-            dw_send(0, 1)
             dw_send(1, 0)
             dw_send(1, 1)
 
@@ -1757,7 +1776,7 @@
             both = dw_mine[which, band, :].astype(F32)
             for step in range(1, far):
                 both = both + dw_across[which, step - 1, band, :].astype(F32)
-            dw_own[which, band, :] = both
+            dw_own[which, band, :] = both.astype(BF)
             return 0
 
         lax.fori_loop(0, dw_mine.shape[1] // 96, add_all, 0)
@@ -1824,7 +1843,7 @@
             shape_of((rows, model), F32),
             shape_of((4 * width, model), BF),
             shape_of((tall, model), F32),
-            shape_of((2, *shard), F32),
+            shape_of((2, *shard), BF),
         ],
         in_specs=[VMEM] * 12 + [ANY] * 13,
         out_specs=[ANY] * 2 + [VMEM] * 4,
@@ -2009,10 +2028,11 @@
         output,
         width,
         experts,
+        scale,
     )
     w_grads, (up_grad, down_grad) = turned[:4], turned[4:6]
     gain_one_grad, shift_one_grad, gain_two_grad, shift_two_grad = turned[6:10]
-    router_grad, input_grad, output = turned[10:]
+    router_grad, input_grad, output, load = turned[10:]
     return (
         output,
         input_grad,
@@ -2024,7 +2044,7 @@
         router_grad.T,
         up_grad[None],
         down_grad[None],
-        small[4, :experts] * scale,
+        load,
     )
 
 

time: 326 us -> 322 us (0.988)
    pallas_call x1, Pallas kernels: 86.4 us -> 61.7 us  [run_back(): pl.pallas_call(partial(back_body, n_e, n_h, experts, capacity, padded, he...]
    pallas_call x1, Pallas kernels: 90.7 us -> 114 us  [run_experts(): pl.pallas_call(partial(moe_body, size, capacity, padded, per), name='expe...]
where the time goes in v1:
time: 322 us; the launch traced here: 320 us
  Pallas kernels  319 us (99%)
    pallas_call x1, Pallas kernels, run_experts(): pl.pallas_call(partial(moe_body, size, capacity, padded, per), name='expe...  114 us
    pallas_call x1, Pallas kernels, run_tail(): pl.pallas_call(partial(tail_body, n_e, n_h, chunks), name='tail', out_sha...  70.7 us
    pallas_call x1, Pallas kernels, run_front(): pl.pallas_call(partial(front_body, n_e, n_h, experts, capacity, padded, h...  63.3 us
    pallas_call x1, Pallas kernels, run_back(): pl.pallas_call(partial(back_body, n_e, n_h, experts, capacity, padded, he...  61.7 us
    pallas_call x1, Pallas kernels, turn_weights(): pl.pallas_call(partial(turn_body, width, experts, scale), name='turn_weig...  10.1 us

profile of v1, /device:TPU:17, one launch (start us, length us, event | category | flops | bytes accessed | tf_op | source)
XLA Modules:
  0.0 320.3 jit_solution(1048930439472202877)
XLA Ops:
  0.6 63.3 %front.1 = (bf16[4,512,768]{2,1,0:T(8,128)(2,1)}, bf16[576,2048]{1,0:T(8,128)(2,1)}, bf16[4,192,512]{2,1,0:T(8,128)(2,1)}, bf16[4,192,512]{2,1,0:T(8,128)(2,1)},...) custom-call(s32[1,3]{1,0:T(1,128)} %docs.1, ...), custom_call_target="tpu_custom_call" | custom-call | tf_op jit(solution)/shard_map/front/pallas_call | solution.py:546
  63.9 113.7 %experts.1 = (bf16[8,160,768]{2,1,0:T(8,128)(2,1)}, f32[8,8,256]{2,1,0:T(8,128)}, bf16[8,160,768]{2,1,0:T(8,128)(2,1)}, bf16[2,2,768,768]{3,2,1,0:T(8,128)(2,1)}, bf16[1,384,768]{2,1,0:T(8,128)(2,1)}) custom-call(bf16[8,160,768]{2,1,0:T(8,128)(2,1)} %get-tuple-element.66.x_slots, f32[8,8,256]{2,1,0:T(8,128)} %get-tuple-element.67.gate_rows, ...), custom_call_target="tpu_custom_call" | custom-call | flops 36238786560 | bytes 41943040 | tf_op jit(solution)/shard_map/experts/pallas_call | solution.py:954
  177.6 61.7 %back.1 = (bf16[8,160,768]{2,1,0:T(8,128)(2,1)}, bf16[4,512,768]{2,1,0:T(8,128)(2,1)}, f32[512,768]{1,0:T(8,128)}, bf16[768,768]{1,0:T(8,128)(2,1)}, f32[16,768]{1,0:T(8,128)}, /*index=5*/bf16[2,768,768]{2,1,0:T(8,128)(2,1)}) custom-call(s32[512,2]{1,0:T(8,128)} %get-tuple-element.60.ids, s32[512,2]{1,0:T(8,128)} %get-tuple-element.61.slot, ...), custom_call_target="tpu_custom_call" | custom-call | tf_op jit(solution)/shard_map/back/pallas_call | solution.py:1837
  239.3 70.7 %tail.1 = (bf16[512,768]{1,0:T(8,128)(2,1)}, bf16[512,768]{1,0:T(8,128)(2,1)}, bf16[4,8,96,768]{3,2,1,0:T(8,128)(2,1)}, f32[16,768]{1,0:T(8,128)}) custom-call(bf16[4,512,768]{2,1,0:T(8,128)(2,1)} %get-tuple-element.82.dh, bf16[8,96,768]{2,1,0:T(8,128)(2,1)} %bitcast.14, f32[16,768]{1,0:T(8,128)} %get-tuple-element.84.small, bf16[512,768]{1,0:T(8,128)(2,1)} %tokens.3, ...), custom_call_target="tpu_custom_call" | custom-call | tf_op jit(solution)/shard_map/tail/pallas_call | solution.py:1287
  310.0 10.1 %turn_weights.1 = (f32[768,768]{1,0:T(8,128)}, f32[768,768]{1,0:T(8,128)}, f32[768,768]{1,0:T(8,128)}, f32[768,768]{1,0:T(8,128)}, f32[768,768]{1,0:T(8,128)}, /...) custom-call(bf16[4,768,768]{2,1,0:T(8,128)(2,1)} %bitcast.10, ...), custom_call_target="tpu_custom_call" | custom-call | bytes 25165824 | tf_op jit(solution)/shard_map/turn_weights/pallas_call | solution.py:1390

commit v2 on v1

--- a/solution.py
+++ b/solution.py
@@ -668,12 +668,16 @@
     steps = size // per
 
     middle = size // 2
+    inner = lax.rem((me // 2 * 8 // size + 1) // 2, 2)
+
+    def group_at(step):
+        late = jnp.where(step <= steps // 2, step - 1 + steps // 2, step - steps // 2)
+        return jnp.where((inner == 1) & (step > 0), late, step)
 
     def peer_at(p):
-        mask = jnp.where(p < 2, p, jnp.where(p < 2 + middle, p - 2 + middle, p - middle))
         peer, bit = 0, 1
         while bit < size:
-            peer = peer + lax.rem(me // bit + mask // bit, 2) * bit
+            peer = peer + lax.rem(me // bit + p // bit, 2) * bit
             bit *= 2
         return peer
 
@@ -739,9 +743,20 @@
         [{"expert": lax.rem(me + step, size)} for step in range(1, size)]
         + [{"hidden": lax.rem(h + step, shards_n)} for step in range(1, shards_n)]
     )
-    for p in range(1, middle):
-        send_x(p).start()
-        send_gate(p).start()
+
+    def send_all(order):
+        for p in order:
+            send_x(p).start()
+            send_gate(p).start()
+
+    @pl.when(inner == 1)
+    def _far_first():
+        send_all([1, *range(middle, size), *range(2, middle)])
+
+    @pl.when(inner == 0)
+    def _near_first():
+        send_all(range(1, size))
+
     for k in range(2):
         for t in range(1, far):
             down_across(t, k).start()
@@ -752,7 +767,8 @@
     load_down.wait()
 
     def step_body(step, _):
-        base = step * per
+        group = group_at(step)
+        base = group * per
         for s in range(per):
 
             @pl.when(base + s > 0)
@@ -761,7 +777,7 @@
                 send_gate(base + s).wait_recv()
 
             load_g(base + s).wait()
-        rows = pl.ds(pl.multiple_of(step * tall, tall), tall)
+        rows = pl.ds(pl.multiple_of(group * tall, tall), tall)
         x, g = xv[rows, :], gv[rows, :]
         y_acc[...] = jnp.zeros_like(y_acc)
         dx_acc[...] = jnp.zeros_like(dx_acc)
@@ -774,15 +790,6 @@
             @pl.when((step == 0) & (n == 1))
             def _beside():
                 down_beside.wait_recv()
-
-            @pl.when((step == 0) & (n == 2))
-            def _second_half():
-                for p in range(1, middle):
-                    send_x(p).wait_send()
-                    send_gate(p).wait_send()
-                for p in range(middle, size):
-                    send_x(p).start()
-                    send_gate(p).start()
 
             @pl.when((step == 0) & (n >= 2) & (beside == 0))
             def _across():
@@ -874,58 +881,60 @@
         source = (up_v, down_v)[which].at[lax.rem(pair + step, far) * 2 + core]
         return pltpu.make_async_copy(source, dw_sum.at[which, step], save_sem.at[which, step])
 
-    def cross(step):
-        source = up_v.at[lax.rem(pair + step, far) * 2 + core, half(0)]
-        there = {"hidden": lax.rem(pair + step, far) * 2 + core}
-        return remote(source, dw_far.at[step - 1], df_s.at[step], df_r.at[step], there)
-
-    def other_body(n, _):
-        band, step = lax.rem(n, bands), lax.rem(n // bands + 1, far)
-        c = lax.rem(pair + step, far) * 2 + 1 - core
+    def cross(step, k):
+        there = lax.rem(pair + step, far) * 2 + core
+        return remote(
+            up_v.at[there, half(k)],
+            dw_far.at[step - 1, half(k)],
+            df_s.at[step, k],
+            df_r.at[step, k],
+            {"hidden": there},
+        )
+
+    def gradients(n, _):
+        band, kind = lax.rem(n, bands), lax.rem(n // bands, 2)
+        step = lax.rem(n // (2 * bands) + 1, far)
+        c = lax.rem(pair + step, far) * 2 + lax.rem(core + 1 + kind, 2)
         lines = aligned(band * turn, turn)
-        up_v[c, lines, :] = mm(xg_t[lines, :], dz[c]).astype(BF)
-        down_v[c, lines, :] = mm(dy_t[lines, :], act[c]).astype(BF)
-
-        @pl.when(band == bands - 1)
+        up = mm(xg_t[lines, :], dz[c])
+        down = mm(dy_t[lines, :], act[c])
+
+        @pl.when(kind == 0)
+        def _other():
+            up_v[c, lines, :] = up.astype(BF)
+            down_v[c, lines, :] = down.astype(BF)
+
+        @pl.when((kind == 0) & (band == bands - 1))
         def _give():
             for which in range(2):
                 give(which, step).start()
 
-        return 0
-
-    lax.fori_loop(0, far * bands, other_body, 0)
-
-    def own_body(n, _):
-        band, step = lax.rem(n, bands), lax.rem(n // bands + 1, far)
-        c = lax.rem(pair + step, far) * 2 + core
-
-        @pl.when(band == 0)
+        @pl.when((kind == 1) & (band == 0))
         def _take():
             for which in range(2):
                 give(which, step).wait_recv()
 
-        lines = aligned(band * turn, turn)
-        up = mm(xg_t[lines, :], dz[c]) + dw_box[0, step, lines, :].astype(F32)
-        down = mm(dy_t[lines, :], act[c]) + dw_box[1, step, lines, :].astype(F32)
-        up_v[c, lines, :] = up.astype(BF)
-        down_v[c, lines, :] = down.astype(BF)
-
-        @pl.when(band == bands - 1)
+        @pl.when(kind == 1)
+        def _own():
+            up_v[c, lines, :] = (up + dw_box[0, step, lines, :].astype(F32)).astype(BF)
+            down_v[c, lines, :] = (down + dw_box[1, step, lines, :].astype(F32)).astype(BF)
+
+        @pl.when((kind == 1) & (band == bands - 1))
         def _keep():
             for which in range(2):
                 keep(which, step).start()
 
-        @pl.when((band == bands - 1) & (step > 0))
+        @pl.when((kind == 1) & (band == bands - 1) & (step > 0))
         def _cross():
-            cross(step).start()
+            for k in range(2):
+                cross(step, k).start()
 
         return 0
 
-    lax.fori_loop(0, far * bands, own_body, 0)
-    for p in range(middle, size):
+    lax.fori_loop(0, 2 * far * bands, gradients, 0)
+    for p in range(1, size):
         send_x(p).wait_send()
         send_gate(p).wait_send()
-    for p in range(1, size):
         send_dx(p).wait()
         send_dg(p).wait()
     for p in range(size):
@@ -937,7 +946,8 @@
             give(which, step).wait_send()
             keep(which, step).wait()
     for step in range(1, far):
-        cross(step).wait()
+        for k in range(2):
+            cross(step, k).wait()
 
 
 def run_experts(x_slots, gate_rows, g_in, ups, w_down, cid):
@@ -959,7 +969,7 @@
             shape_of(gate_rows.shape, F32),
             shape_of(x_slots.shape, BF),
             shape_of((2, shards_n // 2, model, width), BF),
-            shape_of((shards_n // 2 - 1, model // 2, width), BF),
+            shape_of((shards_n // 2 - 1, model, width), BF),
         ],
         in_specs=[ANY] * 5,
         out_specs=[ANY] * 5,
@@ -991,8 +1001,8 @@
             DMA((shards_n // 2, 2)),
             DMA((2, shards_n // 2)),
             DMA((2, shards_n // 2)),
-            DMA((shards_n // 2,)),
-            DMA((shards_n // 2,)),
+            DMA((shards_n // 2, 2)),
+            DMA((shards_n // 2, 2)),
             DMA((size,)),
             DMA((4,)),
         ]
@@ -1024,6 +1034,11 @@
     output,
     full,
     total,
+    wv,
+    tok_v,
+    d_res_v,
+    res_v,
+    yv,
     mine,
     beside,
     across,
@@ -1035,6 +1050,7 @@
     small_mid,
     small_h,
     small_e,
+    load_sem,
     mine_sem,
     cs_sem,
     cr_sem,
@@ -1067,7 +1083,7 @@
         [{"expert": lax.rem(e + step, n_e)} for step in range(1, n_e)]
         + [{"hidden": lax.rem(h + step, n_h)} for step in range(1, n_h)]
     )
-    w_sends, w_order = [], list(range(1, high)) + [0]
+    w_sends, w_order = {}, list(range(1, high)) + [0]
     for step in w_order:
         there = lax.rem(eh + step, high)
         copy = remote(
@@ -1078,7 +1094,7 @@
             {"expert": eh * 2 + 1 - el},
         )
         copy.start()
-        w_sends.append(copy)
+        w_sends[step] = copy
     rows = dh.shape[1] // chunks
     core_sends = {}
     for step in list(range(1, far)) + [0]:
@@ -1094,33 +1110,21 @@
             )
             copy.start()
             core_sends[step, k] = copy
-    loads = []
+    mine_loads = []
     for step in range(far):
         there = lax.rem(pair + step, far)
         load = pltpu.make_async_copy(dh.at[there * 2 + core], mine.at[step], mine_sem.at[step])
         load.start()
-        loads.append(load)
-    small_sends = []
-    for at in range(n_h - 1):
-        peer = lax.rem(h + 1 + at, n_h)
-        copy = remote(small, small_h.at[at], hs_sem.at[at], hr_sem.at[at], {"hidden": peer})
-        copy.start()
-        small_sends.append(copy)
-    v_sends = []
-    for at, step in enumerate(w_order[:-1]):
-        there = lax.rem(eh + step, high) * 2 + el
-        w_sends[at].wait_recv()
-        w_mid[step - 1] = (w_all[there].astype(F32) + x_box[step].astype(F32)).astype(BF)
-        copy = remote(
-            w_mid.at[step - 1],
-            z_box.at[step - 1],
-            vs_sem.at[step],
-            vr_sem.at[step],
-            {"expert": there},
+        mine_loads.append(load)
+    loads = [
+        pltpu.make_async_copy(source, target, load_sem.at[n])
+        for n, (source, target) in enumerate(
+            ((w_all, wv), (residual, res_v), (y_back, yv), (tokens, tok_v), (d_res, d_res_v))
         )
-        copy.start()
-        v_sends.append(copy)
+    ]
     for load in loads:
+        load.start()
+    for load in mine_loads:
         load.wait()
     far_sends = []
     for step in range(1, far):
@@ -1139,6 +1143,121 @@
             )
             copy.start()
             far_sends.append(copy)
+    loads[0].wait()
+    v_sends = []
+    for step in w_order[:-1]:
+        there = lax.rem(eh + step, high) * 2 + el
+        w_sends[step].wait_recv()
+        w_mid[step - 1] = (wv[there].astype(F32) + x_box[step].astype(F32)).astype(BF)
+        copy = remote(
+            w_mid.at[step - 1],
+            z_box.at[step - 1],
+            vs_sem.at[step],
+            vr_sem.at[step],
+            {"expert": there},
+        )
+        copy.start()
+        v_sends.append(copy)
+    small_sends = []
+    for at in range(n_h - 1):
+        peer = lax.rem(h + 1 + at, n_h)
+        copy = remote(small, small_h.at[at], hs_sem.at[at], hr_sem.at[at], {"hidden": peer})
+        copy.start()
+        small_sends.append(copy)
+    w_sends[0].wait_recv()
+    acc = wv[e].astype(F32) + x_box[0].astype(F32)
+    for at, copy in enumerate(v_sends):
+        copy.wait_recv()
+        acc = acc + z_box[at].astype(F32)
+    piece[...] = acc.astype(BF)
+    keep = pltpu.make_async_copy(piece, full.at[h, e], keep_sem)
+    keep.start()
+    started = []
+
+    def slot(eh_of, el_of, pair_of, core_of):
+        return full.at[pair_of * 2 + core_of, eh_of * 2 + el_of]
+
+    def back(step, size, place):
+        return lax.rem(place + size - step, size)
+
+    def give_z(source):
+        for s in range(1, high):
+            there = lax.rem(eh + s, high) * 2 + el
+            copy = remote(
+                source, slot(eh, el, pair, core), zs_sem.at[s], zr_sem.at[s], {"expert": there}
+            )
+            copy.start()
+            started.append(copy)
+
+    def z_arrival(s):
+        place = slot(back(s, high, eh), el, pair, core)
+        return place, remote(place, place, zs_sem.at[s], zr_sem.at[s], {"expert": e})
+
+    def give_x(source, s):
+        target = slot(back(s, high, eh), el, pair, core)
+        copy = remote(
+            source, target, xs_sem.at[s], xr_sem.at[s], {"expert": eh * 2 + 1 - el}
+        )
+        copy.start()
+        started.append(copy)
+
+    def x_arrival(s):
+        place = slot(back(s, high, eh), 1 - el, pair, core)
+        return place, remote(place, place, xs_sem.at[s], xr_sem.at[s], {"expert": e})
+
+    def give_y(source, s, flag):
+        target = slot(back(s, high, eh), el if flag == 0 else 1 - el, pair, core)
+        for t in range(1, far):
+            there = lax.rem(pair + t, far) * 2 + core
+            at = 2 * s + flag
+            copy = remote(
+                source, target, ys_sem.at[t, at], yr_sem.at[t, at], {"hidden": there}
+            )
+            copy.start()
+            started.append(copy)
+
+    def y_arrival(t, s, flag):
+        other = el if flag == 0 else 1 - el
+        place = slot(back(s, high, eh), other, back(t, far, pair), core)
+        at = 2 * s + flag
+        return place, remote(place, place, ys_sem.at[t, at], yr_sem.at[t, at], {"hidden": h})
+
+    def give_mate(source, t, s, flag):
+        other = el if flag == 0 else 1 - el
+        target = slot(back(s, high, eh), other, back(t, far, pair), core)
+        at = 2 * s + flag
+        copy = remote(source, target, ms_sem.at[t, at], mr_sem.at[t, at], {"hidden": mate})
+        copy.start()
+        started.append(copy)
+
+    def mate_arrival(t, s, flag):
+        other = el if flag == 0 else 1 - el
+        place = slot(back(s, high, eh), other, back(t, far, pair), 1 - core)
+        at = 2 * s + flag
+        return place, remote(place, place, ms_sem.at[t, at], mr_sem.at[t, at], {"hidden": h})
+
+    give_z(piece)
+    give_x(piece, 0)
+    give_y(piece, 0, 0)
+    give_mate(piece, 0, 0, 0)
+    arrived = [(0, 0)]
+
+    def take_x(s):
+        place, arrival = x_arrival(s)
+        arrival.wait_recv()
+        give_y(place, s, 1)
+        give_mate(place, 0, s, 1)
+        arrived.append((s, 1))
+
+    for s in range(1, high):
+        place, arrival = z_arrival(s)
+        arrival.wait_recv()
+        give_x(place, s)
+        give_y(place, s, 0)
+        give_mate(place, 0, s, 0)
+        arrived.append((s, 0))
+        take_x(s - 1)
+    take_x(high - 1)
     for copy in small_sends:
         copy.wait_recv()
     summed = small[...]
@@ -1151,105 +1270,14 @@
         copy = remote(small_mid, small_e.at[at], es_sem.at[at], er_sem.at[at], {"expert": peer})
         copy.start()
         small_out.append(copy)
-    w_sends[-1].wait_recv()
-    acc = w_all[e].astype(F32) + x_box[0].astype(F32)
-    for at, copy in enumerate(v_sends):
-        copy.wait_recv()
-        acc = acc + z_box[at].astype(F32)
-    piece[...] = acc.astype(BF)
-    keep = pltpu.make_async_copy(piece, full.at[h, e], keep_sem)
-    keep.start()
-    started = []
-
-    def slot(eh_of, el_of, pair_of, core_of):
-        return full.at[pair_of * 2 + core_of, eh_of * 2 + el_of]
-
-    def back(step, size, place):
-        return lax.rem(place + size - step, size)
-
-    def give_z(source):
-        for s in range(1, high):
-            there = lax.rem(eh + s, high) * 2 + el
-            copy = remote(
-                source, slot(eh, el, pair, core), zs_sem.at[s], zr_sem.at[s], {"expert": there}
-            )
-            copy.start()
-            started.append(copy)
-
-    def z_arrival(s):
-        place = slot(back(s, high, eh), el, pair, core)
-        return place, remote(place, place, zs_sem.at[s], zr_sem.at[s], {"expert": e})
-
-    def give_x(source, s):
-        target = slot(back(s, high, eh), el, pair, core)
-        copy = remote(
-            source, target, xs_sem.at[s], xr_sem.at[s], {"expert": eh * 2 + 1 - el}
-        )
-        copy.start()
-        started.append(copy)
-
-    def x_arrival(s):
-        place = slot(back(s, high, eh), 1 - el, pair, core)
-        return place, remote(place, place, xs_sem.at[s], xr_sem.at[s], {"expert": e})
-
-    def give_y(source, s, flag):
-        target = slot(back(s, high, eh), el if flag == 0 else 1 - el, pair, core)
-        for t in range(1, far):
-            there = lax.rem(pair + t, far) * 2 + core
-            at = 2 * s + flag
-            copy = remote(
-                source, target, ys_sem.at[t, at], yr_sem.at[t, at], {"hidden": there}
-            )
-            copy.start()
-            started.append(copy)
-
-    def y_arrival(t, s, flag):
-        other = el if flag == 0 else 1 - el
-        place = slot(back(s, high, eh), other, back(t, far, pair), core)
-        at = 2 * s + flag
-        return place, remote(place, place, ys_sem.at[t, at], yr_sem.at[t, at], {"hidden": h})
-
-    def give_mate(source, t, s, flag):
-        other = el if flag == 0 else 1 - el
-        target = slot(back(s, high, eh), other, back(t, far, pair), core)
-        at = 2 * s + flag
-        copy = remote(source, target, ms_sem.at[t, at], mr_sem.at[t, at], {"hidden": mate})
-        copy.start()
-        started.append(copy)
-
-    def mate_arrival(t, s, flag):
-        other = el if flag == 0 else 1 - el
-        place = slot(back(s, high, eh), other, back(t, far, pair), 1 - core)
-        at = 2 * s + flag
-        return place, remote(place, place, ms_sem.at[t, at], mr_sem.at[t, at], {"hidden": h})
-
-    give_z(piece)
-    give_x(piece, 0)
-    give_y(piece, 0, 0)
-    give_mate(piece, 0, 0, 0)
-    for s in range(1, high):
-        place, arrival = z_arrival(s)
-        arrival.wait_recv()
-        give_x(place, s)
-        give_y(place, s, 0)
-        give_mate(place, 0, s, 0)
-    for s in range(high):
-        place, arrival = x_arrival(s)
-        arrival.wait_recv()
-        give_y(place, s, 1)
-        give_mate(place, 0, s, 1)
+    for load in loads[1:]:
+        load.wait()
     place_of = iota((residual.shape[0], y_back.shape[0]), 1)
-    result = residual[...]
+    result = res_v[...]
     for j in range(2):
         pick = (place_of == pos[:, j : j + 1]).astype(BF)
-        result = result + gates[:, j : j + 1] * mm(pick, y_back[...])
+        result = result + gates[:, j : j + 1] * mm(pick, yv[...])
     output[...] = result.astype(BF)
-    for copy in small_out:
-        copy.wait_recv()
-    summed = small_mid[...]
-    for at in range(n_e - 1):
-        summed = summed + small_e[at]
-    total[...] = summed
     for k in range(chunks):
         part = pl.ds(k * rows, rows)
         core_sends[0, k].wait_recv()
@@ -1258,21 +1286,25 @@
     grad = mine[0].astype(F32) + beside[0].astype(F32)
     for step in range(far - 1):
         grad = grad + across[step].astype(F32)
-    normed, inverse = norm_parts(tokens[...].astype(F32))
-    input_grad[...] = (d_res[...] + norm_back(grad, normed, inverse, lying(gain))).astype(BF)
+    normed, inverse = norm_parts(tok_v[...].astype(F32))
+    input_grad[...] = (d_res_v[...] + norm_back(grad, normed, inverse, lying(gain))).astype(BF)
     for t in range(1, far):
-        for s in range(high):
-            for flag in range(2):
-                place, arrival = y_arrival(t, s, flag)
-                arrival.wait_recv()
-                give_mate(place, t, s, flag)
+        for s, flag in arrived:
+            place, arrival = y_arrival(t, s, flag)
+            arrival.wait_recv()
+            give_mate(place, t, s, flag)
+    for copy in small_out:
+        copy.wait_recv()
+    summed = small_mid[...]
+    for at in range(n_e - 1):
+        summed = summed + small_e[at]
+    total[...] = summed
     for t in range(far):
-        for s in range(high):
-            for flag in range(2):
-                _place, arrival = mate_arrival(t, s, flag)
-                arrival.wait_recv()
+        for s, flag in arrived:
+            _place, arrival = mate_arrival(t, s, flag)
+            arrival.wait_recv()
     keep.wait()
-    for copy in started + w_sends + v_sends + small_sends + small_out + far_sends:
+    for copy in [*started, *w_sends.values(), *v_sends, *small_sends, *small_out, *far_sends]:
         copy.wait_send()
     for copy in core_sends.values():
         copy.wait_send()
@@ -1293,9 +1325,14 @@
             shape_of((n_h, n_e, *piece), BF),
             shape_of(small.shape, F32),
         ],
-        in_specs=[ANY] + [VMEM] * 9,
+        in_specs=[ANY, ANY, VMEM, ANY, VMEM, ANY, ANY, VMEM, VMEM, ANY],
         out_specs=[VMEM, VMEM, ANY, VMEM],
         scratch_shapes=[
+            pltpu.VMEM(w_all.shape, BF),
+            pltpu.VMEM(tokens.shape, BF),
+            pltpu.VMEM(d_res.shape, F32),
+            pltpu.VMEM(residual.shape, F32),
+            pltpu.VMEM(y_back.shape, BF),
             pltpu.VMEM((far, rows, model), BF),
             pltpu.VMEM((far, rows, model), BF),
             pltpu.VMEM((far - 1, rows, model), BF),
@@ -1307,6 +1344,7 @@
             pltpu.VMEM(small.shape, F32),
             pltpu.VMEM((n_h - 1, *small.shape), F32),
             pltpu.VMEM((n_e - 1, *small.shape), F32),
+            DMA((5,)),
             DMA((far,)),
             DMA((far, chunks)),
             DMA((far, chunks)),
@@ -1552,25 +1590,25 @@
     load_dw.start()
     deep = dw_mine.shape[1] // 2
     load_far = pltpu.make_async_copy(
-        dw_far, dw_across.at[0, :, pl.ds(0, deep)], dw_sem.at[1]
+        dw_far, dw_across.at[0], dw_sem.at[1]
     )
     load_far.start()
 
-    def dw_across_copy(which, step, k):
+    def dw_across_copy(step, k):
         part = pl.ds(k * deep, deep)
         return remote(
-            dw_sum.at[which, step, part],
-            dw_across.at[which, step - 1, part],
-            da_s.at[which, step, k],
-            da_r.at[which, step, k],
+            dw_sum.at[1, step, part],
+            dw_across.at[1, step - 1, part],
+            da_s.at[step, k],
+            da_r.at[step, k],
             {"hidden": lax.rem(pair + step, far) * 2 + core},
         )
 
-    def dw_send(which, k):
+    def dw_send(k):
         for step in range(1, far):
-            dw_across_copy(which, step, k).start()
-
-    dw_send(0, 1)
+            dw_across_copy(step, k).start()
+
+    dw_send(0)
     for step in range(1, n_e):
         peer = lax.rem(e + step, n_e)
         copy = remote(y_out.at[peer], y_back.at[e], y_s.at[step], y_r.at[step], {"expert": peer})
@@ -1701,8 +1739,7 @@
                 both = wo[target].astype(F32) + wo_box[step].astype(F32)
                 wo[target] = both.astype(BF)
                 give_wo(step).start()
-            dw_send(1, 0)
-            dw_send(1, 1)
+            dw_send(1)
 
         load_kept(i, turn).wait()
         cols = aligned(lax.rem(at, per_device) * BLOCK, BLOCK)
@@ -1767,9 +1804,9 @@
     load_dw.wait()
     load_far.wait()
     for which in range(2):
-        for step in range(1, far):
-            for k in range(1 - which, 2):
-                dw_across_copy(which, step, k).wait()
+        for step in range(1, far if which == 1 else 1):
+            for k in range(2):
+                dw_across_copy(step, k).wait()
 
         def add_all(n, _, which=which):
             band = aligned(n * 96, 96)
@@ -1879,7 +1916,7 @@
             *pairs(n_h),
             *pairs(far),
             *pairs(far),
-            *pairs(2, far, 2),
+            *pairs(far, 2),
         ],
         compiler_params=pltpu.CompilerParams(
             collective_id=cid, has_side_effects=True, vmem_limit_bytes=60 << 20

time: 322 us -> 293 us (0.910)
  Pallas kernels: 319 us -> 292 us
    pallas_call x1, Pallas kernels: 61.7 us -> 47.8 us  [run_back(): pl.pallas_call(partial(back_body, n_e, n_h, experts, capacity, padded, he...]
    pallas_call x1, Pallas kernels: 114 us -> 106 us  [run_experts(): pl.pallas_call(partial(moe_body, size, capacity, padded, per), name='expe...]
    pallas_call x1, Pallas kernels: 70.7 us -> 64.6 us  [run_tail(): pl.pallas_call(partial(tail_body, n_e, n_h, chunks), name='tail', out_sha...]
where the time goes in v2:
time: 293 us
  Pallas kernels  292 us (100%)
    pallas_call x1, Pallas kernels, run_experts(): pl.pallas_call(partial(moe_body, size, capacity, padded, per), name='expe...  106 us
    pallas_call x1, Pallas kernels, run_tail(): pl.pallas_call(partial(tail_body, n_e, n_h, chunks), name='tail', out_sha...  64.6 us
    pallas_call x1, Pallas kernels, run_front(): pl.pallas_call(partial(front_body, n_e, n_h, experts, capacity, padded, h...  63.2 us
    pallas_call x1, Pallas kernels, run_back(): pl.pallas_call(partial(back_body, n_e, n_h, experts, capacity, padded, he...  47.8 us
    pallas_call x1, Pallas kernels, turn_weights(): pl.pallas_call(partial(turn_body, width, experts, scale), name='turn_weig...  10.1 us

profile of v2, /device:TPU:17, one launch (start us, length us, event | category | flops | bytes accessed | tf_op | source)
XLA Modules:
  0.0 292.5 jit_solution(14973285899482199585)
XLA Ops:
  0.6 63.2 %front.1 = (bf16[4,512,768]{2,1,0:T(8,128)(2,1)}, bf16[576,2048]{1,0:T(8,128)(2,1)}, bf16[4,192,512]{2,1,0:T(8,128)(2,1)}, bf16[4,192,512]{2,1,0:T(8,128)(2,1)},...) custom-call(s32[1,3]{1,0:T(1,128)} %docs.1, ...), custom_call_target="tpu_custom_call" | custom-call | tf_op jit(solution)/shard_map/front/pallas_call | solution.py:546
  63.9 105.9 %experts.1 = (bf16[8,160,768]{2,1,0:T(8,128)(2,1)}, f32[8,8,256]{2,1,0:T(8,128)}, bf16[8,160,768]{2,1,0:T(8,128)(2,1)}, bf16[2,2,768,768]{3,2,1,0:T(8,128)(2,1)}, bf16[1,768,768]{2,1,0:T(8,128)(2,1)}) custom-call(bf16[8,160,768]{2,1,0:T(8,128)(2,1)} %get-tuple-element.66.x_slots, f32[8,8,256]{2,1,0:T(8,128)} %get-tuple-element.67.gate_rows, ...), custom_call_target="tpu_custom_call" | custom-call | flops 36238786560 | bytes 41943040 | tf_op jit(solution)/shard_map/experts/pallas_call | solution.py:964
  169.8 47.8 %back.1 = (bf16[8,160,768]{2,1,0:T(8,128)(2,1)}, bf16[4,512,768]{2,1,0:T(8,128)(2,1)}, f32[512,768]{1,0:T(8,128)}, bf16[768,768]{1,0:T(8,128)(2,1)}, f32[16,768]{1,0:T(8,128)}, /*index=5*/bf16[2,768,768]{2,1,0:T(8,128)(2,1)}) custom-call(s32[512,2]{1,0:T(8,128)} %get-tuple-element.60.ids, s32[512,2]{1,0:T(8,128)} %get-tuple-element.61.slot, ...), custom_call_target="tpu_custom_call" | custom-call | tf_op jit(solution)/shard_map/back/pallas_call | solution.py:1874
  217.5 64.6 %tail.1 = (bf16[512,768]{1,0:T(8,128)(2,1)}, bf16[512,768]{1,0:T(8,128)(2,1)}, bf16[4,8,96,768]{3,2,1,0:T(8,128)(2,1)}, f32[16,768]{1,0:T(8,128)}) custom-call(bf16[4,512,768]{2,1,0:T(8,128)(2,1)} %get-tuple-element.82.dh, bf16[8,96,768]{2,1,0:T(8,128)(2,1)} %bitcast.14, f32[16,768]{1,0:T(8,128)} %get-tuple-element.84.small, bf16[512,768]{1,0:T(8,128)(2,1)} %tokens.3, ...), custom_call_target="tpu_custom_call" | custom-call | tf_op jit(solution)/shard_map/tail/pallas_call | solution.py:1319
  282.2 10.1 %turn_weights.1 = (f32[768,768]{1,0:T(8,128)}, f32[768,768]{1,0:T(8,128)}, f32[768,768]{1,0:T(8,128)}, f32[768,768]{1,0:T(8,128)}, f32[768,768]{1,0:T(8,128)}, /...) custom-call(bf16[4,768,768]{2,1,0:T(8,128)(2,1)} %bitcast.10, ...), custom_call_target="tpu_custom_call" | custom-call | bytes 25165824 | tf_op jit(solution)/shard_map/turn_weights/pallas_call | solution.py:1428
